TPU v7x, 512 devices: a whole 4x8x8 slice. The times are simulated.
512 devices in a mesh: patch: 128 (over y, z, core), visit: 4 (over x).
Axes of the slice: x: 4, y: 8, z: 8, core: 2. Of those that a mesh axis runs over, the one named last changes fastest.
Arguments:
- pieces: bfloat16 [49152, 32, 128], P(('patch', 'visit')), may hold values from -16 to 16
- dest: int32 [49152, 1], P(('patch', 'visit')), may hold values from 0 to 127; in each aligned block of 96 rows (0 to 95, 96 to 191, ...) at most 2 rows name the same one
- offsets: int32 [49152], P(('patch', 'visit')), may hold values from 0 to 224
- kernel_index: int32 [49152], P(('patch', 'visit')), may hold values from 0 to 39
- weights: bfloat16 [49152], P(('patch', 'visit')), may hold values from 0.25 to 4
- basis_col: bfloat16 [14, 41], replicated, may hold values from -1 to 1
- basis_row: bfloat16 [14, 41], replicated, may hold values from -1 to 1
- coef_table: float32 [40, 14], replicated, may hold values from -2.4 to 2.4
- det_taps: bfloat16 [2, 21], replicated, may hold values from -1.25 to 1.25
Outputs:
- coadd: float32 [32768, 128], P(('patch', 'visit'))
- detection: float32 [32768, 128], P(('patch', 'visit'))
Inputs may be any that keep to these rules, and one draw needn't show every extreme that they name: `dest`: at most 2 of the pieces of one device intersect one patch.
All inputs are finite; a program needn't handle non-finite values.
Results may differ from a plain program's by a relative error of at most 0.0062.
Values may be sent and summed in bfloat16 or wider, within the bound.
A program may use at most 64 MiB of HBM per device.

v0:
```python
from functools import partial
import math

import jax
import jax.numpy as jnp
from jax import lax
from jax.sharding import PartitionSpec as P

PH = 256


def extended_2(x, sides, width):
    for axis, dim in sides:
        devices, length = (lax.axis_size(axis), x.shape[dim])
        up = [(i, (i + 1) % devices) for i in range(devices - 1)]
        down = [(j, i) for i, j in up]
        last = lax.slice_in_dim(x, length - width, length, axis=dim)
        initial = lax.slice_in_dim(x, 0, width, axis=dim)
        before = lax.ppermute(last, axis, up)
        after = lax.ppermute(initial, axis, down)
        x = jnp.concatenate([before, x, after], axis=dim)
    return x


def banded(tap_table, height, columns, center):
    offsets_grid = jnp.arange(columns)[None, :] - jnp.arange(height)[:, None] + center
    one_hot = (offsets_grid[:, :, None] == jnp.arange(tap_table.shape[1])[None, None, :]).astype(
        jnp.bfloat16
    )
    return jnp.einsum("ijt,bt->bij", one_hot, tap_table, preferred_element_type=jnp.float32).astype(
        jnp.bfloat16
    )


def match_block(operands, col_bands, row_bands):
    images, factors = operands
    stacked = jnp.einsum(
        "nrk,bkc->nbrc", images, col_bands, preferred_element_type=jnp.float32
    ).astype(jnp.bfloat16)
    number, basis_count, height, columns = stacked.shape
    stacked = stacked.reshape(number, basis_count * height, columns)
    row_kernel = factors[:, None, :, None] * row_bands.astype(jnp.float32).transpose(1, 0, 2)[None]
    row_kernel = row_kernel.reshape(number, height, basis_count * height).astype(jnp.bfloat16)
    matched = jnp.einsum("nrq,nqc->nrc", row_kernel, stacked, preferred_element_type=jnp.float32)
    return matched.astype(jnp.bfloat16)


def match_all(images, kind_ids, coef_table, col_bands, row_bands):
    number = images.shape[0]
    block_size = math.gcd(number, 32)
    one_hot = (kind_ids[:, None] == jnp.arange(coef_table.shape[0])[None, :]).astype(jnp.float32)
    factors = jnp.dot(one_hot, coef_table, precision=lax.Precision.HIGHEST)
    grouped = (
        images.reshape((number // block_size, block_size) + images.shape[1:]),
        factors.reshape(number // block_size, block_size, factors.shape[1]),
    )
    matched = lax.map(partial(match_block, col_bands=col_bands, row_bands=row_bands), grouped)
    return matched.reshape(images.shape)


def place_bulk(slot_hot, values):
    flat = values.reshape(values.shape[0], -1)
    placed = jnp.dot(slot_hot.astype(jnp.bfloat16), flat, preferred_element_type=jnp.float32)
    return placed.astype(jnp.bfloat16).reshape((slot_hot.shape[0],) + values.shape[1:])


def place_ints(slot_hot, values):
    placed = jnp.dot(slot_hot, values.astype(jnp.float32), precision=lax.Precision.HIGHEST)
    return placed.astype(jnp.int32)


def shards(
    pieces, dest, offsets, kernel_index, weights, basis_col, basis_row, coef_table, det_taps
):
    patches = lax.axis_size("patch")
    local_count = pieces.shape[0]
    capacity = max(2, 2 * local_count // patches)
    piece_rows = pieces.shape[1]
    columns = pieces.shape[2]
    half_taps = basis_col.shape[1] // 2
    col_bands = banded(basis_col, columns, columns, half_taps)
    row_bands = banded(basis_row, piece_rows, piece_rows, half_taps)
    targets = dest[:, 0]
    position = jnp.arange(local_count)
    before = (position[None, :] < position[:, None]) & (targets[None, :] == targets[:, None])
    earlier = jnp.sum(before.astype(jnp.int32), axis=1)
    slots = targets * capacity + earlier
    total_slots = patches * capacity
    slot_hot = (jnp.arange(total_slots)[:, None] == slots[None, :]).astype(jnp.float32)
    sent_weights = place_bulk(slot_hot, weights[:, None])[:, 0]
    pairs = jnp.stack([offsets, kernel_index], axis=1)
    sent_pairs = place_ints(slot_hot, pairs)
    outgoing = place_bulk(slot_hot, pieces)
    arrived, arrived_weights, arrived_pairs = (
        lax.all_to_all(outgoing, "patch", split_axis=0, concat_axis=0, tiled=True),
        lax.all_to_all(sent_weights, "patch", split_axis=0, concat_axis=0, tiled=True),
        lax.all_to_all(sent_pairs, "patch", split_axis=0, concat_axis=0, tiled=True),
    )
    matched = match_all(arrived, arrived_pairs[:, 1], coef_table, col_bands, row_bands)
    arrived_starts = arrived_pairs[:, 0]
    row_index = (arrived_starts[:, None] + jnp.arange(piece_rows)[None, :]).reshape(-1)
    repeated = jnp.repeat(arrived_weights, piece_rows)
    placement = jnp.where(
        jnp.arange(PH)[:, None] == row_index[None, :],
        repeated[None, :],
        jnp.zeros((), jnp.bfloat16),
    )
    numerator = jnp.dot(placement, matched.reshape(-1, columns), preferred_element_type=jnp.float32)
    denominator = jnp.sum(placement.astype(jnp.float32), axis=1)
    det_half = det_taps.shape[1] // 2
    det_cols = banded(det_taps[1:2], columns, columns, det_half)[0]
    numerator, denominator = (
        lax.psum_scatter(numerator, "visit", scatter_dimension=0, tiled=True),
        lax.psum_scatter(denominator, "visit", scatter_dimension=0, tiled=True),
    )
    coadd = numerator / (1.0 + denominator)[:, None]
    smoothed = jnp.dot(
        coadd.astype(jnp.bfloat16), det_cols, preferred_element_type=jnp.float32
    ).astype(jnp.bfloat16)
    extended = extended_2(smoothed, (("visit", 0),), det_half)
    strip_length = coadd.shape[0]
    row_filter = banded(det_taps[0:1], strip_length, strip_length + 2 * det_half, 0)[0]
    detection = jnp.dot(row_filter, extended, preferred_element_type=jnp.float32)
    return (coadd, detection)


def solution(mesh):
    in_specs = (
        P(("patch", "visit"), None, None),
        P(("patch", "visit"), None),
        P(("patch", "visit")),
        P(("patch", "visit")),
        P(("patch", "visit")),
        P(),
        P(),
        P(),
        P(),
    )
    out_specs = (P(("patch", "visit"), None), P(("patch", "visit"), None))
    return jax.shard_map(shards, mesh=mesh, in_specs=in_specs, out_specs=out_specs, check_vma=False)
```

profile of v0, /device:TPU:56, one launch (start us, length us, event | category | flops | bytes accessed | tf_op | source)
XLA Modules:
  0.0 210.4 jit_solution(14648906646209383570)
XLA Ops:
  10.4 17.3 %all-to-all-start.1 = ((bf16[128,2,1]{1,2,0:T(2,128)(2,1)}), bf16[128,2,1]{1,2,0:T(2,128)(2,1)S(1)}, u32[]{:S(2)}, u32[]{:S(2)}) async-start(bf16[128,2,1]{1,2,0:T(2,128)(2,1)} %all_to_all.26), calls=%async_computation.1 | async-start | bytes 131072 | tf_op jit(solution)/shard_map/all_to_all | solution.py:96
  29.5 7.7 %all-to-all-done.1 = bf16[128,2,1]{1,2,0:T(2,128)(2,1)S(1)} async-done(((bf16[128,2,1]{1,2,0:T(2,128)(2,1)}), bf16[128,2,1]{1,2,0:T(2,128)(2,1)S(1)}, u32[]{:S(2)}, u32[]{:S(2)}) %all-to-all-start.1) | async-done | bytes 544 | tf_op jit(solution)/shard_map/all_to_all | solution.py:96
  37.2 7.8 %all-to-all-start = ((s32[128,2,2]{1,2,0:T(2,128)}), s32[128,2,2]{1,2,0:T(2,128)S(1)}, u32[]{:S(2)}, u32[]{:S(2)}) async-start(s32[128,2,2]{1,2,0:T(2,128)} %copy.25), calls=%async_computation | async-start | bytes 262144 | tf_op jit(solution)/shard_map/all_to_all | solution.py:97
  48.7 7.1 %all-to-all-done = s32[128,2,2]{1,2,0:T(2,128)S(1)} async-done(((s32[128,2,2]{1,2,0:T(2,128)}), s32[128,2,2]{1,2,0:T(2,128)S(1)}, u32[]{:S(2)}, u32[]{:S(2)}) %all-to-all-start) | async-done | bytes 2080 | tf_op jit(solution)/shard_map/all_to_all | solution.py:97
  55.8 7.9 %all-to-all-start.2 = ((bf16[256,32,128]{2,1,0:T(8,128)(2,1)}), bf16[256,32,128]{2,1,0:T(8,128)(2,1)S(1)}, u32[]{:S(2)}, u32[]{:S(2)}) async-start(bf16[256,32,128]{2,1,0:T(8,128)(2,1)} %bitcast.41), calls=%async_computation.2 | async-start | bytes 4194304 | tf_op jit(solution)/shard_map/all_to_all | solution.py:95
  69.4 45.2 %all-to-all-done.2 = bf16[256,32,128]{2,1,0:T(8,128)(2,1)S(1)} async-done(((bf16[256,32,128]{2,1,0:T(8,128)(2,1)}), bf16[256,32,128]{2,1,0:T(8,128)(2,1)S(1)}, u32[]{:S(2)}, u32[]{:S(2)}) %all-to-all-start.2) | async-done | bytes 2097184 | tf_op jit(solution)/shard_map/all_to_all | solution.py:95
  114.6 55.1 %while.10 = (s32[]{:T(128)}, bf16[8,32,32,128]{3,2,1,0:T(8,128)(2,1)}, f32[8,32,14]{2,1,0:T(8,128)S(1)}, bf16[14,32,32]{2,0,1:T(8,128)(2,1)S(1)}, bf16[8,32,32,1...) while((s32[]{:T(128)}, bf16[8,32,32,128]{3,2,1,0:T(8,128)(2,1)}, ...), condition=%wide.region_2.3_spmd, body=%wide.region_1.2_spmd.sunk | while | flops 590100480 | bytes 8816469 | solution.py:57
  114.6 2.9 %convolution_convert_fusion.7 = bf16[32,32,14,128]{3,1,2,0:T(8,128)(2,1)} fusion(bf16[14,128,128]{2,1,0:T(8,128)(2,1)S(1)} %get-tuple-element.137, bf16[8,32,32,128]{3,2,1,0:T(8,128)(2,1)S(1)} %get-tuple-element.136, s32[]{:T(128)} %get-tuple-element.125), kind=kOutput, calls=%fused_computation.clone.1 | convolution fusion | flops 471597056 | bytes 4390916 | tf_op jit(solution)/shard_map/while/body/eval_jaxpr/nrk,bkc->nbrc/dot_general | solution.py:37
  117.9 3.6 %fusion.65 = bf16[8,32,32,128]{3,2,1,0:T(8,128)(2,1)} fusion(bf16[8,32,32,128]{3,2,1,0:T(8,128)(2,1)} %get-tuple-element.126, s32[]{:T(128)} %get-tuple-element.125, bf16[32,448,128]{2,1,0:T(8,128)(2,1)} %bitcast.86, f32[32,448]{1,0:T(8,128)S(1)} %reshape.142, f32[32,448]{1,0:T(8,128)S(1)} %mul.62), kind=kOutput, calls=%fused_computation.4.clone.1 | convolution fusion | flops 118489088 | bytes 4047360 | tf_op jit(solution)/shard_map/while/body/eval_jaxpr/nrq,nqc->nrc/dot_general | solution.py:44
  121.5 2.9 %convolution_convert_fusion.7 = bf16[32,32,14,128]{3,1,2,0:T(8,128)(2,1)} fusion(bf16[14,128,128]{2,1,0:T(8,128)(2,1)S(1)} %get-tuple-element.137, bf16[8,32,32,128]{3,2,1,0:T(8,128)(2,1)S(1)} %get-tuple-element.136, s32[]{:T(128)} %get-tuple-element.125), kind=kOutput, calls=%fused_computation.clone.1 | convolution fusion | flops 471597056 | bytes 4390916 | tf_op jit(solution)/shard_map/while/body/eval_jaxpr/nrk,bkc->nbrc/dot_general | solution.py:37
  124.8 3.6 %fusion.65 = bf16[8,32,32,128]{3,2,1,0:T(8,128)(2,1)} fusion(bf16[8,32,32,128]{3,2,1,0:T(8,128)(2,1)} %get-tuple-element.126, s32[]{:T(128)} %get-tuple-element.125, bf16[32,448,128]{2,1,0:T(8,128)(2,1)} %bitcast.86, f32[32,448]{1,0:T(8,128)S(1)} %reshape.142, f32[32,448]{1,0:T(8,128)S(1)} %mul.62), kind=kOutput, calls=%fused_computation.4.clone.1 | convolution fusion | flops 118489088 | bytes 4047360 | tf_op jit(solution)/shard_map/while/body/eval_jaxpr/nrq,nqc->nrc/dot_general | solution.py:44
  131.7 3.6 %fusion.65 = bf16[8,32,32,128]{3,2,1,0:T(8,128)(2,1)} fusion(bf16[8,32,32,128]{3,2,1,0:T(8,128)(2,1)} %get-tuple-element.126, s32[]{:T(128)} %get-tuple-element.125, bf16[32,448,128]{2,1,0:T(8,128)(2,1)} %bitcast.86, f32[32,448]{1,0:T(8,128)S(1)} %reshape.142, f32[32,448]{1,0:T(8,128)S(1)} %mul.62), kind=kOutput, calls=%fused_computation.4.clone.1 | convolution fusion | flops 118489088 | bytes 4047360 | tf_op jit(solution)/shard_map/while/body/eval_jaxpr/nrq,nqc->nrc/dot_general | solution.py:44
  138.5 3.6 %fusion.65 = bf16[8,32,32,128]{3,2,1,0:T(8,128)(2,1)} fusion(bf16[8,32,32,128]{3,2,1,0:T(8,128)(2,1)} %get-tuple-element.126, s32[]{:T(128)} %get-tuple-element.125, bf16[32,448,128]{2,1,0:T(8,128)(2,1)} %bitcast.86, f32[32,448]{1,0:T(8,128)S(1)} %reshape.142, f32[32,448]{1,0:T(8,128)S(1)} %mul.62), kind=kOutput, calls=%fused_computation.4.clone.1 | convolution fusion | flops 118489088 | bytes 4047360 | tf_op jit(solution)/shard_map/while/body/eval_jaxpr/nrq,nqc->nrc/dot_general | solution.py:44
  142.1 2.9 %convolution_convert_fusion.7 = bf16[32,32,14,128]{3,1,2,0:T(8,128)(2,1)} fusion(bf16[14,128,128]{2,1,0:T(8,128)(2,1)S(1)} %get-tuple-element.137, bf16[8,32,32,128]{3,2,1,0:T(8,128)(2,1)S(1)} %get-tuple-element.136, s32[]{:T(128)} %get-tuple-element.125), kind=kOutput, calls=%fused_computation.clone.1 | convolution fusion | flops 471597056 | bytes 4390916 | tf_op jit(solution)/shard_map/while/body/eval_jaxpr/nrk,bkc->nbrc/dot_general | solution.py:37
  145.4 3.6 %fusion.65 = bf16[8,32,32,128]{3,2,1,0:T(8,128)(2,1)} fusion(bf16[8,32,32,128]{3,2,1,0:T(8,128)(2,1)} %get-tuple-element.126, s32[]{:T(128)} %get-tuple-element.125, bf16[32,448,128]{2,1,0:T(8,128)(2,1)} %bitcast.86, f32[32,448]{1,0:T(8,128)S(1)} %reshape.142, f32[32,448]{1,0:T(8,128)S(1)} %mul.62), kind=kOutput, calls=%fused_computation.4.clone.1 | convolution fusion | flops 118489088 | bytes 4047360 | tf_op jit(solution)/shard_map/while/body/eval_jaxpr/nrq,nqc->nrc/dot_general | solution.py:44
  149.0 2.9 %convolution_convert_fusion.7 = bf16[32,32,14,128]{3,1,2,0:T(8,128)(2,1)} fusion(bf16[14,128,128]{2,1,0:T(8,128)(2,1)S(1)} %get-tuple-element.137, bf16[8,32,32,128]{3,2,1,0:T(8,128)(2,1)S(1)} %get-tuple-element.136, s32[]{:T(128)} %get-tuple-element.125), kind=kOutput, calls=%fused_computation.clone.1 | convolution fusion | flops 471597056 | bytes 4390916 | tf_op jit(solution)/shard_map/while/body/eval_jaxpr/nrk,bkc->nbrc/dot_general | solution.py:37
  152.3 3.6 %fusion.65 = bf16[8,32,32,128]{3,2,1,0:T(8,128)(2,1)} fusion(bf16[8,32,32,128]{3,2,1,0:T(8,128)(2,1)} %get-tuple-element.126, s32[]{:T(128)} %get-tuple-element.125, bf16[32,448,128]{2,1,0:T(8,128)(2,1)} %bitcast.86, f32[32,448]{1,0:T(8,128)S(1)} %reshape.142, f32[32,448]{1,0:T(8,128)S(1)} %mul.62), kind=kOutput, calls=%fused_computation.4.clone.1 | convolution fusion | flops 118489088 | bytes 4047360 | tf_op jit(solution)/shard_map/while/body/eval_jaxpr/nrq,nqc->nrc/dot_general | solution.py:44
  155.9 2.9 %convolution_convert_fusion.7 = bf16[32,32,14,128]{3,1,2,0:T(8,128)(2,1)} fusion(bf16[14,128,128]{2,1,0:T(8,128)(2,1)S(1)} %get-tuple-element.137, bf16[8,32,32,128]{3,2,1,0:T(8,128)(2,1)S(1)} %get-tuple-element.136, s32[]{:T(128)} %get-tuple-element.125), kind=kOutput, calls=%fused_computation.clone.1 | convolution fusion | flops 471597056 | bytes 4390916 | tf_op jit(solution)/shard_map/while/body/eval_jaxpr/nrk,bkc->nbrc/dot_general | solution.py:37
  159.3 3.5 %fusion.65 = bf16[8,32,32,128]{3,2,1,0:T(8,128)(2,1)} fusion(bf16[8,32,32,128]{3,2,1,0:T(8,128)(2,1)} %get-tuple-element.126, s32[]{:T(128)} %get-tuple-element.125, bf16[32,448,128]{2,1,0:T(8,128)(2,1)} %bitcast.86, f32[32,448]{1,0:T(8,128)S(1)} %reshape.142, f32[32,448]{1,0:T(8,128)S(1)} %mul.62), kind=kOutput, calls=%fused_computation.4.clone.1 | convolution fusion | flops 118489088 | bytes 4047360 | tf_op jit(solution)/shard_map/while/body/eval_jaxpr/nrq,nqc->nrc/dot_general | solution.py:44
  166.1 3.6 %fusion.65 = bf16[8,32,32,128]{3,2,1,0:T(8,128)(2,1)} fusion(bf16[8,32,32,128]{3,2,1,0:T(8,128)(2,1)} %get-tuple-element.126, s32[]{:T(128)} %get-tuple-element.125, bf16[32,448,128]{2,1,0:T(8,128)(2,1)} %bitcast.86, f32[32,448]{1,0:T(8,128)S(1)} %reshape.142, f32[32,448]{1,0:T(8,128)S(1)} %mul.62), kind=kOutput, calls=%fused_computation.4.clone.1 | convolution fusion | flops 118489088 | bytes 4047360 | tf_op jit(solution)/shard_map/while/body/eval_jaxpr/nrq,nqc->nrc/dot_general | solution.py:44
  169.7 3.5 %fusion.9 = f32[256,128]{1,0:T(8,128)} fusion(bf16[8192,128]{1,0:T(8,128)(2,1)} %bitcast.94, s32[8192]{0:T(1024)S(1)} %add.77, bf16[8192]{0:T(1024)(128)(2,1)S(1)} %broadcast_in_dim.21), kind=kOutput, calls=%fused_computation.16 | convolution fusion | flops 541065216 | bytes 2277376 | tf_op jit(solution)/shard_map/dot_general | solution.py:108
  174.8 10.5 %all-reduce = f32[256]{0:T(256)S(1)} all-reduce(f32[256]{0:T(256)S(1)} %convert_reduce_fusion), channel_id=3, replica_groups=mesh['patch'=128,'visit'=4] {'visit'}, use_global_device_ids=true, to_apply=%region_5.6.clone | all-reduce | flops 256 | bytes 2048
  185.4 9.4 %reduce-scatter.2.cloned.1.call-done = f32[64,128]{1,0:T(8,128)} async-done(((f32[256,128]{1,0:T(8,128)}), f32[64,128]{1,0:T(8,128)}) %reduce-scatter.2.cloned.1.call-update) | async-done | bytes 32784 | tf_op jit(solution)/shard_map/reduce_scatter | solution.py:113
  198.9 3.9 %collective-permute-done.1 = bf16[10,128]{1,0:T(8,128)(2,1)S(1)} collective-permute-done((bf16[10,128]{1,0:T(8,128)(2,1)S(1)}, bf16[10,128]{1,0:T(8,128)(2,1)S(1)}, u32[]{:S(2)}, u32[]{:S(2)}) %collective-permute-start.1) | collective-permute-done | bytes 2592 | tf_op jit(solution)/shard_map/ppermute | solution.py:20
  (97 shorter events, 32.0 us)
Async XLA Ops:
  7.2 62.0 %copy-start = (f32[40,14]{0,1:T(8,128)S(1)}, f32[40,14]{0,1:T(8,128)}, u32[]{:S(2)}) copy-start(f32[40,14]{0,1:T(8,128)} %param.18) | copy-start | bytes 6724
  10.4 26.8 %all-to-all-start.1 = ((bf16[128,2,1]{1,2,0:T(2,128)(2,1)}), bf16[128,2,1]{1,2,0:T(2,128)(2,1)S(1)}, u32[]{:S(2)}, u32[]{:S(2)}) async-start(bf16[128,2,1]{1,2,0:T(2,128)(2,1)} %all_to_all.26), calls=%async_computation.1 | async-start | bytes 131072 | tf_op jit(solution)/shard_map/all_to_all | solution.py:96
  37.2 18.6 %all-to-all-start = ((s32[128,2,2]{1,2,0:T(2,128)}), s32[128,2,2]{1,2,0:T(2,128)S(1)}, u32[]{:S(2)}, u32[]{:S(2)}) async-start(s32[128,2,2]{1,2,0:T(2,128)} %copy.25), calls=%async_computation | async-start | bytes 262144 | tf_op jit(solution)/shard_map/all_to_all | solution.py:97
  55.7 8.2 %copy-start.2 = (bf16[14,41]{1,0:T(8,128)(2,1)S(1)}, bf16[14,41]{1,0:T(8,128)(2,1)}, u32[]{:S(2)}) copy-start(bf16[14,41]{1,0:T(8,128)(2,1)} %param.16) | copy-start | bytes 3448
  55.8 11.0 %copy-start.3 = (bf16[14,41]{1,0:T(8,128)(2,1)S(1)}, bf16[14,41]{1,0:T(8,128)(2,1)}, u32[]{:S(2)}) copy-start(bf16[14,41]{1,0:T(8,128)(2,1)} %param.17) | copy-start | bytes 3448
  55.8 58.9 %all-to-all-start.2 = ((bf16[256,32,128]{2,1,0:T(8,128)(2,1)}), bf16[256,32,128]{2,1,0:T(8,128)(2,1)S(1)}, u32[]{:S(2)}, u32[]{:S(2)}) async-start(bf16[256,32,128]{2,1,0:T(8,128)(2,1)} %bitcast.41), calls=%async_computation.2 | async-start | bytes 4194304 | tf_op jit(solution)/shard_map/all_to_all | solution.py:95
  63.7 3.9 %copy-start.4 = (bf16[2,21]{1,0:T(2,128)(2,1)S(1)}, bf16[2,21]{1,0:T(2,128)(2,1)}, u32[]{:S(2)}) copy-start(bf16[2,21]{1,0:T(2,128)(2,1)} %param.19) | copy-start | bytes 256
  63.7 131.1 %reduce-scatter.2.cloned.1.call-start = ((), (), s32[]{:S(2)}) async-start(), calls=%async_computation.4 | async-start | bytes 163840 | tf_op jit(solution)/shard_map/reduce_scatter | solution.py:113
  195.6 8.0 %copy-start.1 = (f32[64,128]{1,0:T(8,128)}, f32[64,128]{1,0:T(8,128)S(1)}, u32[]{:S(2)}) copy-start(f32[64,128]{1,0:T(8,128)S(1)} %broadcast_divide_fusion) | copy-start | bytes 98308
  195.7 3.1 %collective-permute-start = (bf16[10,128]{1,0:T(8,128)(2,1)S(1)}, bf16[10,128]{1,0:T(8,128)(2,1)S(1)}, u32[]{:S(2)}, u32[]{:S(2)}) collective-permute-start(bf16[10,128]{1,0:T(8,128)(2,1)S(1)} %get-tuple-element.77), channel_id=1, source_target_pairs={{0,1},{1,2},{2,3},{4,5},{5,6},{6,7},{8,9},{9,10},{10,11},{12,13},{... | collective-permute-start | bytes 7688 | tf_op jit(solution)/shard_map/ppermute | solution.py:19
  197.3 5.5 %collective-permute-start.1 = (bf16[10,128]{1,0:T(8,128)(2,1)S(1)}, bf16[10,128]{1,0:T(8,128)(2,1)S(1)}, u32[]{:S(2)}, u32[]{:S(2)}) collective-permute-start(bf16[10,128]{1,0:T(8,128)(2,1)S(1)} %get-tuple-element.78), channel_id=1, source_target_pairs={{1,0},{2,1},{3,2},{5,4},{6,5},{7,6},{9,8},{10,9},{11,10},{13,12},{... | collective-permute-start | bytes 7688 | tf_op jit(solution)/shard_map/ppermute | solution.py:20
Sparse Core Ops, SparseCore 0:
  173.3 21.3 reduce-scatter.1
where the time goes:
time: 212 us; the launch traced here: 210 us
  waiting for transfers between devices  73.3 us (35%)
  matrix products  61.8 us (29%)
  starting transfers between devices  36.1 us (17%)
  between operations  14.9 us (7%)
  blocking collectives  10.5 us (5%)
  local copies, waits for them, and re-layouts  8.74 us (4%)
  other arithmetic  4.88 us (2%)
    all_to_all x1, waiting for transfers between devices, shards(): lax.all_to_all(outgoing, 'patch', split_axis=0, concat_axis=0, tiled=True)  45.2 us
    dot_general x8, matrix products, match_block(): jnp.einsum('nrq,nqc->nrc', row_kernel, stacked, preferred_element_type=jn...  28.5 us
    dot_general x8, matrix products, match_block(): jnp.einsum('nrk,bkc->nbrc', images, col_bands, preferred_element_type=jnp...  23.1 us
    all_to_all x1, starting transfers between devices, shards(): lax.all_to_all(sent_weights, 'patch', split_axis=0, concat_axis=0, tiled=...  17.3 us
    unnamed x1, blocking collectives  10.5 us
    reduce_scatter x1, waiting for transfers between devices, shards(): lax.psum_scatter(numerator, 'visit', scatter_dimension=0, tiled=True)  9.4 us
    all_to_all x1, starting transfers between devices, shards(): lax.all_to_all(outgoing, 'patch', split_axis=0, concat_axis=0, tiled=True)  7.92 us
    all_to_all x1, starting transfers between devices, shards(): lax.all_to_all(sent_pairs, 'patch', split_axis=0, concat_axis=0, tiled=True)  7.82 us
  transfers between devices with their start and end apart: 6, of which 5 were waited for; matrix products, arithmetic and copies ran while one was open for 6% of the time, Pallas kernels for 0%

commit v1 on v0

v1 whole, which is shorter than its diff:
```python
import functools

import jax
import jax.numpy as jnp
from jax import lax
from jax.experimental import pallas as pl
from jax.experimental.pallas import tpu as pltpu
from jax.sharding import PartitionSpec as P

MESH = pl.DeviceIdType.MESH
F32 = jnp.float32
BF16 = jnp.bfloat16

PIECES = 96
PR = 32
PW = 128
PH = 256
TAPS = 41
NB = 14
TD = 21
SIDE = 8
VISITS = 4
GROUP = 16
STRIP = PH // VISITS
HALO = 16
CHUNKS = 2
CHUNK_SLOTS = 16 // CHUNKS
CHUNK_DESTS = 8 // CHUNKS


def iota(shape, axis):
    return lax.broadcasted_iota(jnp.int32, shape, axis)


def match_kernel(
    dest_s, off_s, kind_s, weight_s, coef_s, col_ref, row_ref, x_ref,
    data_ref, meta_ref,
    g_ref, r_ref, y_ref, pad_ref, mt_ref, mw_ref, count_s,
):
    half = TAPS // 2
    pad_ref[...] = jnp.zeros_like(pad_ref)
    pad_ref[0:NB, 4 : 4 + TAPS] = col_ref[...].astype(F32)
    pad_ref[16 : 16 + NB, 4 : 4 + TAPS] = row_ref[...].astype(F32)
    band = jnp.abs(iota((PW, PW), 1) - iota((PW, PW), 0)) <= half
    row_lane = iota((PR, PW), 1)
    row_band = (jnp.abs(row_lane - iota((PR, PW), 0)) <= half) & (row_lane < PR)
    for b in range(NB):
        taps = jnp.broadcast_to(pad_ref[b : b + 1, :], (PW, PW))
        g = pltpu.roll(taps, PW - half - 4, 1, stride=1, stride_axis=0)
        g_ref[b * PW : (b + 1) * PW, :] = jnp.where(band, g, 0.0).astype(BF16)
        taps = jnp.broadcast_to(pad_ref[16 + b : 17 + b, :], (PR, PW))
        r = pltpu.roll(taps, PW - half - 4, 1, stride=1, stride_axis=0)
        r = jnp.where(row_band, r, 0.0)
        r = r + pltpu.roll(r, 32, 1) + pltpu.roll(r, 64, 1) + pltpu.roll(r, 96, 1)
        r_ref[b] = r.reshape(4, 8, PW)

    data_ref[...] = jnp.zeros_like(data_ref)
    mt_ref[...] = jnp.zeros_like(mt_ref)
    mw_ref[...] = jnp.zeros_like(mw_ref)

    @pl.loop(0, 128)
    def _(d):
        count_s[d] = 0

    lane8 = iota((8, PW), 1)
    lane1 = iota((1, PW), 1)
    step = (lane1 % 32).astype(F32)
    which = (lane1 // 32) % 2
    zeros = jnp.zeros((PR, PW), BF16)

    @pl.loop(0, PIECES // GROUP)
    def _(group):
        first = group * GROUP
        for quad in range(GROUP // 4):
            kinds = [kind_s[first + quad * 4 + j] for j in range(4)]
            parts = []
            for b in range(NB):
                factor = jnp.where(
                    lane8 < 64,
                    jnp.where(lane8 < 32, coef_s[kinds[0], b], coef_s[kinds[1], b]),
                    jnp.where(lane8 < 96, coef_s[kinds[2], b], coef_s[kinds[3], b]),
                )
                parts.append((r_ref[b] * factor[None]).reshape(PR, PW))
            row_kernel = jnp.concatenate(parts, axis=0).astype(BF16)
            x = [x_ref[first + quad * 4 + j] for j in range(4)]
            for pair in range(2):
                rows = []
                for j in range(4):
                    left = x[j] if j == 2 * pair else zeros
                    right = x[j] if j == 2 * pair + 1 else zeros
                    rows.append(jnp.concatenate([left, right], axis=1))
                both = jnp.concatenate(rows, axis=0)
                y = jnp.dot(row_kernel, both, preferred_element_type=F32).astype(BF16)
                for j in range(2):
                    at = (quad * 4 + pair * 2 + j) * PR
                    for b in range(NB):
                        y_ref[at : at + PR, b * PW : (b + 1) * PW] = y[
                            b * PR : (b + 1) * PR, j * PW : (j + 1) * PW
                        ]
        matched = jnp.dot(y_ref[...], g_ref[...], preferred_element_type=F32).astype(BF16)
        for j in range(GROUP):
            n = first + j
            d = dest_s[n]
            k = count_s[d]
            count_s[d] = k + 1
            y_to = d // 16
            z_to = (d // 2) % 8
            c_to = d % 2
            message = jnp.where(c_to == 0, z_to, 8 + y_to)
            inner = jnp.where(c_to == 0, y_to, z_to)
            row = message * 8 + inner
            data_ref[row * 2 + k] = matched[j * PR : (j + 1) * PR, :]
            mine = which == k
            mt_ref[pl.ds(row, 1), :] = jnp.where(
                mine, off_s[n].astype(F32) + step, mt_ref[pl.ds(row, 1), :]
            )
            mw_ref[pl.ds(row, 1), :] = jnp.where(mine, weight_s[n], mw_ref[pl.ds(row, 1), :])

    meta_ref[...] = jnp.concatenate(
        [mt_ref[...].reshape(16, 8, PW), mw_ref[...].reshape(16, 8, PW)], axis=1
    ).astype(BF16)


def exchange_kernel(
    data_ref, meta_ref, taps_ref,
    coadd_ref, detection_ref,
    rb, mb, mf, sb, rbb, sc, rc, den_ref, pad_ref, d_ref, f_ref,
    meta_send, meta_recv, a_send, a_recv, b_send, b_recv, c_send, c_recv,
):
    p = lax.axis_index("patch")
    v = lax.axis_index("visit")
    c = lax.rem(p, 2)
    z = lax.rem(p // 2, SIDE)
    y = p // (2 * SIDE)
    along = jnp.where(c == 0, y, z)

    def patch_of(y_at, z_at, c_at):
        return (y_at * SIDE + z_at) * 2 + c_at

    barrier = pltpu.get_barrier_semaphore()

    def greet(target):
        pl.semaphore_signal(barrier, inc=1, device_id={"patch": target}, device_id_type=MESH)

    @pl.loop(1, SIDE)
    def _(i):
        for core in range(2):
            greet(patch_of(y, lax.rem(z + i, SIDE), core))
            greet(patch_of(lax.rem(y + i, SIDE), z, core))

    greet(patch_of(y, z, 1 - c))

    @pl.loop(1, VISITS)
    def _(i):
        pl.semaphore_signal(
            barrier, inc=1, device_id={"visit": lax.rem(v + i, VISITS)}, device_id_type=MESH
        )

    half = TD // 2
    pad_ref[...] = jnp.zeros_like(pad_ref)
    pad_ref[0:2, 6 : 6 + TD] = taps_ref[...].astype(F32)
    cols = pltpu.roll(jnp.broadcast_to(pad_ref[1:2, :], (PW, PW)), PW - half - 6, 1, stride=1, stride_axis=0)
    d_ref[...] = jnp.where(
        jnp.abs(iota((PW, PW), 1) - iota((PW, PW), 0)) <= half, cols, 0.0
    ).astype(BF16)
    rows = pltpu.roll(
        jnp.broadcast_to(pad_ref[0:1, :], (STRIP, PW)), HALO - half - 6, 1, stride=1, stride_axis=0
    )
    f_ref[...] = rows.astype(BF16)

    pl.semaphore_wait(barrier, 4 * (SIDE - 1) + 1 + VISITS - 1)

    def meta_copy(message, slot, target):
        return pltpu.make_async_remote_copy(
            src_ref=meta_ref.at[message], dst_ref=mb.at[slot],
            send_sem=meta_send.at[message], recv_sem=meta_recv.at[slot],
            device_id={"patch": target}, device_id_type=MESH,
        )

    def chunk_of(message, part):
        return data_ref.at[pl.ds(message * 16 + part * CHUNK_SLOTS, CHUNK_SLOTS)]

    def slots_of(slot, part):
        return rb.at[slot, pl.ds(part * CHUNK_SLOTS, CHUNK_SLOTS)]

    def a_copy(message, part, slot, target):
        return pltpu.make_async_remote_copy(
            src_ref=chunk_of(message, part), dst_ref=slots_of(slot, part),
            send_sem=a_send.at[part, message], recv_sem=a_recv.at[part, slot],
            device_id={"patch": target}, device_id_type=MESH,
        )

    z_slot = z * 2 + c
    y_slot = y * 2 + c
    here = jnp.where(c == 0, z, 8 + y)
    here_slot = jnp.where(c == 0, z_slot, y_slot)
    other = jnp.where(c == 0, 8 + y, z)
    other_slot = jnp.where(c == 0, y_slot, z_slot)
    partner = patch_of(y, z, 1 - c)

    pltpu.make_async_copy(meta_ref.at[here], mb.at[here_slot], meta_recv.at[here_slot]).start()
    meta_copy(other, other_slot, partner).start()

    @pl.loop(1, SIDE)
    def _(i):
        z_to = lax.rem(z + i, SIDE)
        y_to = lax.rem(y + i, SIDE)
        meta_copy(z_to, z_slot, patch_of(y, z_to, 0)).start()
        meta_copy(8 + y_to, y_slot, patch_of(y_to, z, 1)).start()

    for part in range(CHUNKS):

        @pl.loop(1, SIDE)
        def _(i):
            z_to = lax.rem(z + i, SIDE)
            y_to = lax.rem(y + i, SIDE)
            a_copy(z_to, part, z_slot, patch_of(y, z_to, 0)).start()
            a_copy(8 + y_to, part, y_slot, patch_of(y_to, z, 1)).start()

        a_copy(other, part, other_slot, partner).start()
        pltpu.make_async_copy(
            chunk_of(here, part), slots_of(here_slot, part), a_recv.at[part, here_slot]
        ).start()

    @pl.loop(0, 16)
    def _(s):
        meta_copy(s, s, partner).wait_recv()

    mf[...] = mb[...].astype(F32)

    row_f = iota((PH, PW), 0).astype(F32)
    low = iota((1, PW), 1) < 64
    eye = iota((PW, PW), 0) == iota((PW, PW), 1)
    tile_row = iota((16, PW), 0)
    ones = jnp.ones((4 * 64, PW), BF16)

    def b_copy(j):
        return pltpu.make_async_remote_copy(
            src_ref=sb.at[j], dst_ref=rbb.at[along],
            send_sem=b_send.at[j], recv_sem=b_recv.at[along],
            device_id={"patch": jnp.where(c == 0, patch_of(j, z, 0), patch_of(y, j, 1))},
            device_id_type=MESH,
        )

    for part in range(CHUNKS):

        @pl.loop(0, 16)
        def _(s):
            a_copy(s, part, s, partner).wait_recv()

        @pl.loop(part * CHUNK_DESTS, (part + 1) * CHUNK_DESTS)
        def _(j):
            total = jnp.zeros((PH, 2 * PW), F32)
            for four in range(4):
                places = []
                blocks = []
                for pair in range(2):
                    s = four * 4 + pair * 2
                    t = jnp.where(low, mf[s, pl.ds(j, 1), :], mf[s + 1, pl.ds(j, 1), :])
                    w = jnp.where(low, mf[s, pl.ds(8 + j, 1), :], mf[s + 1, pl.ds(8 + j, 1), :])
                    places.append(jnp.where(row_f == t, w, 0.0).astype(BF16))
                    for k in range(2):
                        blocks.append(rb[s + k, pl.ds(2 * j, 2)].reshape(64, PW))
                place = jnp.concatenate(places, axis=1)
                block = jnp.concatenate([jnp.concatenate(blocks, axis=0), ones], axis=1)
                total = total + jnp.dot(place, block, preferred_element_type=F32)
            sb[j, 0:PH, :] = total[:, 0:PW].astype(BF16)
            d0 = jnp.sum(jnp.where(eye, total[0:PW, PW:], 0.0), axis=0, keepdims=True)
            d1 = jnp.sum(jnp.where(eye, total[PW:, PW:], 0.0), axis=0, keepdims=True)
            h0 = d0.astype(BF16).astype(F32)
            h1 = d1.astype(BF16).astype(F32)
            tile = jnp.where(tile_row == 0, h0, jnp.where(tile_row == 1, h1, 0.0))
            tile = jnp.where(tile_row == 8, d0 - h0, jnp.where(tile_row == 9, d1 - h1, tile))
            sb[j, PH : PH + 16, :] = tile.astype(BF16)

            @pl.when(j == along)
            def _():
                pltpu.make_async_copy(sb.at[j], rbb.at[along], b_recv.at[along]).start()

            @pl.when(j != along)
            def _():
                b_copy(j).start()

    num = jnp.zeros((PH, PW), F32)
    den = jnp.zeros((8, PW), F32)
    for i in range(SIDE):
        pltpu.make_async_copy(rbb.at[i], rbb.at[i], b_recv.at[i]).wait()
        num = num + rbb[i, 0:PH, :].astype(F32)
        tile = rbb[i, PH : PH + 16, :].astype(F32)
        den = den + (tile[0:8] + tile[8:16])

    edge = jnp.zeros((HALO, PW), F32)
    for x in range(VISITS):
        start = x * STRIP - HALO
        stop = start + STRIP + 2 * HALO
        if x == 0:
            strip = jnp.concatenate([edge, num[0:stop]], axis=0)
        elif x == VISITS - 1:
            strip = jnp.concatenate([num[start:PH], edge], axis=0)
        else:
            strip = num[start:stop]
        sc[x, 0 : STRIP + 2 * HALO, :] = strip
        sc[x, STRIP + 2 * HALO :, :] = den

    def c_copy(x):
        return pltpu.make_async_remote_copy(
            src_ref=sc.at[x], dst_ref=rc.at[v], send_sem=c_send.at[x], recv_sem=c_recv.at[v],
            device_id={"visit": x}, device_id_type=MESH,
        )

    @pl.loop(1, VISITS)
    def _(i):
        c_copy(lax.rem(v + i, VISITS)).start()

    pltpu.make_async_copy(sc.at[v], rc.at[v], c_recv.at[v]).start()

    total = jnp.zeros((STRIP + 2 * HALO, PW), F32)
    den = jnp.zeros((8, PW), F32)
    for i in range(VISITS):
        pltpu.make_async_copy(rc.at[i], rc.at[i], c_recv.at[i]).wait()
        total = total + rc[i, 0 : STRIP + 2 * HALO, :]
        den = den + rc[i, STRIP + 2 * HALO :, :]

    den_ref[...] = jnp.zeros_like(den_ref)
    for a in range(2):
        spread = jnp.where(eye, jnp.broadcast_to(den[a : a + 1, :], (PW, PW)), 0.0)
        column = jnp.sum(spread, axis=1, keepdims=True)
        den_ref[HALO + a * PW : HALO + (a + 1) * PW, :] = jnp.broadcast_to(column, (PW, PW))
    mine = den_ref[pl.ds(pl.multiple_of(v * STRIP, STRIP), STRIP + 2 * HALO), :]
    coadd = total / (1.0 + mine)
    coadd_ref[...] = coadd[HALO : HALO + STRIP]
    smoothed = jnp.dot(coadd.astype(BF16), d_ref[...], preferred_element_type=F32).astype(BF16)
    smoothed = jnp.concatenate([smoothed, jnp.zeros((PW - STRIP - 2 * HALO, PW), BF16)], axis=0)
    detection_ref[...] = jnp.dot(f_ref[...], smoothed, preferred_element_type=F32)

    meta_copy(other, other_slot, partner).wait_send()

    @pl.loop(1, SIDE)
    def _(i):
        meta_copy(lax.rem(z + i, SIDE), z_slot, partner).wait_send()
        meta_copy(8 + lax.rem(y + i, SIDE), y_slot, partner).wait_send()

    for part in range(CHUNKS):
        a_copy(other, part, other_slot, partner).wait_send()

        @pl.loop(1, SIDE)
        def _(i):
            a_copy(lax.rem(z + i, SIDE), part, z_slot, partner).wait_send()
            a_copy(8 + lax.rem(y + i, SIDE), part, y_slot, partner).wait_send()

    @pl.loop(0, SIDE)
    def _(j):
        @pl.when(j != along)
        def _():
            b_copy(j).wait_send()

    @pl.loop(1, VISITS)
    def _(i):
        c_copy(lax.rem(v + i, VISITS)).wait_send()


def match(pieces, dest, offsets, kernel_index, weights, basis_col, basis_row, coef_table):
    smem = pl.BlockSpec(memory_space=pltpu.SMEM)
    vmem = pl.BlockSpec(memory_space=pltpu.VMEM)
    return pl.pallas_call(
        match_kernel,
        out_shape=(
            jax.ShapeDtypeStruct((256, PR, PW), BF16),
            jax.ShapeDtypeStruct((16, 16, PW), BF16),
        ),
        in_specs=[smem] * 5 + [vmem] * 3,
        out_specs=(vmem, vmem),
        scratch_shapes=[
            pltpu.VMEM((NB * PW, PW), BF16),
            pltpu.VMEM((NB, 4, 8, PW), F32),
            pltpu.VMEM((GROUP * PR, NB * PW), BF16),
            pltpu.VMEM((32, PW), F32),
            pltpu.VMEM((128, PW), F32),
            pltpu.VMEM((128, PW), F32),
            pltpu.SMEM((128,), jnp.int32),
        ],
        name="match",
    )(dest[:, 0], offsets, kernel_index, weights.astype(F32), coef_table, basis_col, basis_row, pieces)


def exchange(data, meta, det_taps):
    hbm = pl.BlockSpec(memory_space=pl.ANY)
    vmem = pl.BlockSpec(memory_space=pltpu.VMEM)
    dma = pltpu.SemaphoreType.DMA
    out = jax.ShapeDtypeStruct((STRIP, PW), F32)
    return pl.pallas_call(
        exchange_kernel,
        out_shape=(out, out),
        in_specs=[hbm, hbm, vmem],
        out_specs=(vmem, vmem),
        scratch_shapes=[
            pltpu.VMEM((16, 16, PR, PW), BF16),
            pltpu.VMEM((16, 16, PW), BF16),
            pltpu.VMEM((16, 16, PW), F32),
            pltpu.VMEM((SIDE, PH + 16, PW), BF16),
            pltpu.VMEM((SIDE, PH + 16, PW), BF16),
            pltpu.VMEM((VISITS, STRIP + 2 * HALO + 8, PW), F32),
            pltpu.VMEM((VISITS, STRIP + 2 * HALO + 8, PW), F32),
            pltpu.VMEM((PH + 2 * HALO, PW), F32),
            pltpu.VMEM((8, PW), F32),
            pltpu.VMEM((PW, PW), BF16),
            pltpu.VMEM((STRIP, PW), BF16),
            dma((16,)),
            dma((16,)),
            dma((CHUNKS, 16)),
            dma((CHUNKS, 16)),
            dma((SIDE,)),
            dma((SIDE,)),
            dma((VISITS,)),
            dma((VISITS,)),
        ],
        compiler_params=pltpu.CompilerParams(collective_id=0, has_side_effects=True),
        name="exchange",
    )(data, meta, det_taps)


def shards(
    pieces, dest, offsets, kernel_index, weights, basis_col, basis_row, coef_table, det_taps
):
    data, meta = match(
        pieces, dest, offsets, kernel_index, weights, basis_col, basis_row, coef_table
    )
    return exchange(data, meta, det_taps)


def solution(mesh):
    split = P(("patch", "visit"))
    in_specs = (
        P(("patch", "visit"), None, None),
        P(("patch", "visit"), None),
        split,
        split,
        split,
        P(),
        P(),
        P(),
        P(),
    )
    out_specs = (P(("patch", "visit"), None), P(("patch", "visit"), None))
    return jax.shard_map(shards, mesh=mesh, in_specs=in_specs, out_specs=out_specs, check_vma=False)
```

time: 212 us -> 77.4 us (0.37)
  the two profiles are of different devices: /device:TPU:56 before, /device:TPU:184 now
where the time goes in v1:
time: 77.4 us; the launch traced here: 77.1 us
  Pallas kernels  71.1 us (92%)
  local copies, waits for them, and re-layouts  4.13 us (5%)
  other arithmetic  1.17 us (2%)
    pallas_call x1, Pallas kernels, exchange(): pl.pallas_call(exchange_kernel, out_shape=(out, out), in_specs=[hbm, hbm,...  59.1 us
    pallas_call x1, Pallas kernels, match(): pl.pallas_call(match_kernel, out_shape=(jax.ShapeDtypeStruct((256, PR, PW...  12 us
    unnamed x3, local copies, waits for them, and re-layouts  4.13 us

profile of v1, /device:TPU:184, one launch (start us, length us, event | category | flops | bytes accessed | tf_op | source)
XLA Modules:
  0.0 77.1 jit_solution(2147730927767277196)
XLA Ops:
  0.6 1.2 %convert_element_type.3.weight_s = f32[96]{0:T(128)} convert(bf16[96]{0:T(256)(128)(2,1)} %param.13) | non-fusion elementwise | flops 96 | bytes 576 | tf_op jit(solution)/shard_map/convert_element_type | solution.py:383
  1.8 1.4 %copy.11.coef_s = f32[40,14]{1,0:T(8,128)} copy(f32[40,14]{0,1:T(8,128)} %param.16) | data formatting | bytes 4480 | tf_op args[7]
  3.2 12.0 %match.1 = (bf16[256,32,128]{2,1,0:T(8,128)(2,1)}, bf16[16,16,128]{2,1,0:T(8,128)(2,1)}) custom-call(s32[96]{0:T(128)} %bitcast.1, s32[96]{0:T(128)} %off_s.1, s32[96]{0:T(128)} %kind_s.1, f32[96]{0:T(128)} %convert_element_type.3.weight_s, f32[40,14]{1,0:T(8,128)} %copy.11.coef_s, bf16[14,41]{1,0:T(8,128)(2,1)} %col_ref.1, bf16[14,41]{1,0:T(8,128)(2,1)} %row_ref.1, ...), custom_call_target="tpu_custom_call" | custom-call | tf_op jit(solution)/shard_map/match/pallas_call | solution.py:365
  15.2 59.1 %exchange.1 = (f32[64,128]{1,0:T(8,128)}, f32[64,128]{1,0:T(8,128)}) custom-call(bf16[256,32,128]{2,1,0:T(8,128)(2,1)} %get-tuple-element.4.data_ref, bf16[16,16,128]{2,1,0:T(8,128)(2,1)} %get-tuple-element.5.meta_ref, bf16[2,21]{1,0:T(2,128)(2,1)} %taps_ref.1), custom_call_target="tpu_custom_call" | custom-call | tf_op jit(solution)/shard_map/exchange/pallas_call | solution.py:391
  74.3 1.4 %copy.14 = f32[64,128]{1,0:T(8,128)} copy(f32[64,128]{1,0:T(8,128)} %get-tuple-element.8) | data formatting | bytes 65536
  75.7 1.4 %copy.15 = f32[64,128]{1,0:T(8,128)} copy(f32[64,128]{1,0:T(8,128)} %get-tuple-element.9) | data formatting | bytes 65536

commit v2 on v1

v2 whole, which is shorter than its diff:
```python
import functools

import jax
import jax.numpy as jnp
from jax import lax
from jax.experimental import pallas as pl
from jax.experimental.pallas import tpu as pltpu
from jax.sharding import PartitionSpec as P

MESH = pl.DeviceIdType.MESH
F32 = jnp.float32
BF16 = jnp.bfloat16
I32 = jnp.int32

PIECES = 96
PR = 32
PW = 128
PH = 256
TAPS = 41
NB = 14
TD = 21
SIDE = 8
VISITS = 4
GROUP = 16
STRIP = PH // VISITS
HALO = 16
SPAN = STRIP + 2 * HALO
SLOTS = 16
META = 16
ROWS = META + SLOTS * PR
CHUNKS = 2
CHUNK_DESTS = 8 // CHUNKS
ORDER = (3, 5, 4, 2, 6, 1, 7, 0)


def iota(shape, axis):
    return lax.broadcasted_iota(I32, shape, axis)


def chosen(index, values):
    result = jnp.full_like(index, values[-1])
    for at, value in enumerate(values[:-1]):
        result = jnp.where(index == at, value, result)
    return result


def tables(col_ref, row_ref, pad_ref, g_ref, r_ref):
    half = TAPS // 2
    pad_ref[...] = jnp.zeros_like(pad_ref)
    pad_ref[0:NB, 4 : 4 + TAPS] = col_ref[...].astype(F32)
    pad_ref[16 : 16 + NB, 4 : 4 + TAPS] = row_ref[...].astype(F32)
    band = jnp.abs(iota((PW, PW), 1) - iota((PW, PW), 0)) <= half
    row_lane = iota((PR, PW), 1)
    row_band = (jnp.abs(row_lane - iota((PR, PW), 0)) <= half) & (row_lane < PR)
    for b in range(NB):
        taps = jnp.broadcast_to(pad_ref[b : b + 1, :], (PW, PW))
        g = pltpu.roll(taps, PW - half - 4, 1, stride=1, stride_axis=0)
        g_ref[b * PW : (b + 1) * PW, :] = jnp.where(band, g, 0.0).astype(BF16)
        taps = jnp.broadcast_to(pad_ref[16 + b : 17 + b, :], (PR, PW))
        r = pltpu.roll(taps, PW - half - 4, 1, stride=1, stride_axis=0)
        r = jnp.where(row_band, r, 0.0)
        r = r + pltpu.roll(r, 32, 1) + pltpu.roll(r, 64, 1) + pltpu.roll(r, 96, 1)
        r_ref[b] = r.reshape(4, 8, PW)


def plan(y, z, dest_ref, off_ref, weight_ref, plan_ref, padf_ref, stage_ref):
    plan_ref[...] = jnp.full_like(plan_ref, -1)
    plan_ref[0:1, 0:PIECES] = dest_ref[...]
    padf_ref[...] = jnp.zeros_like(padf_ref)
    padf_ref[0:1, 0:PIECES] = off_ref[...].astype(F32)
    padf_ref[1:2, 0:PIECES] = weight_ref[...].astype(F32)
    square = (PW, PW)
    lane, row = iota(square, 1), iota(square, 0)
    d = jnp.broadcast_to(plan_ref[0:1, :], square)
    d_t = d.T
    earlier = jnp.sum(jnp.where((d == d_t) & (row < lane), 1, 0), axis=0, keepdims=True)
    d1 = plan_ref[0:1, :]
    y_to, z_to, c_to = d1 >> 4, (d1 >> 1) & 7, d1 & 1
    distance = jnp.where(c_to == 0, z_to - z, y_to - y) & 7
    inner = jnp.where(c_to == 0, y_to, z_to)
    turn = chosen(distance, tuple(ORDER.index(o) for o in range(SIDE)))
    position = ((turn * 2 + c_to) * 8 + inner) * 2 + earlier
    lane1 = iota((1, PW), 1)
    position = jnp.where(lane1 < PIECES, position, 1024 + lane1)
    pos = jnp.broadcast_to(position, square)
    pos_t = pos.T
    rank = jnp.sum(jnp.where(pos_t < pos, 1, 0), axis=0, keepdims=True)
    rank_t = jnp.broadcast_to(rank, square).T
    order = jnp.sum(jnp.where(rank_t == lane, row, 0), axis=0, keepdims=True)
    plan_ref[0:1, :] = order
    for a in range(2):
        plan_ref[1 + a : 2 + a, :] = PIECES + jnp.sum(
            jnp.where(pos_t == lane + a * PW, rank_t - PIECES, 0), axis=0, keepdims=True
        )
    which = (lane // PR) & 1
    hot = jnp.concatenate(
        [jnp.where(pos == 2 * row + k, 1.0, 0.0).astype(BF16) for k in range(2)], axis=1
    )
    found = []
    for at in range(2):
        value = jnp.broadcast_to(padf_ref[at : at + 1, :], square).T
        value = jnp.concatenate(
            [jnp.where(which == k, value, 0.0).astype(BF16) for k in range(2)], axis=0
        )
        found.append(jnp.dot(hot, value, preferred_element_type=F32))
    target = found[0] + (lane & (PR - 1)).astype(F32)
    stage_ref[:, 0:META, :] = jnp.concatenate(
        [target.reshape(16, 8, PW), found[1].reshape(16, 8, PW)], axis=1
    ).astype(BF16)


def match_group(group, kind_s, coef_s, plan_s, x, r_ref, g_ref, y_ref, matched_ref):
    first = group * GROUP
    lane8 = iota((8, PW), 1)
    zeros = jnp.zeros((PR, PW), BF16)
    for quad in range(GROUP // 4):
        pieces = [plan_s[0, first + quad * 4 + j] for j in range(4)]
        kinds = [kind_s[n] for n in pieces]
        parts = []
        for b in range(NB):
            factor = jnp.where(
                lane8 < 64,
                jnp.where(lane8 < 32, coef_s[b, kinds[0]], coef_s[b, kinds[1]]),
                jnp.where(lane8 < 96, coef_s[b, kinds[2]], coef_s[b, kinds[3]]),
            )
            parts.append((r_ref[b] * factor[None]).reshape(PR, PW))
        row_kernel = jnp.concatenate(parts, axis=0).astype(BF16)
        images = [x[n] for n in pieces]
        for pair in range(2):
            rows = []
            for j in range(4):
                left = images[j] if j == 2 * pair else zeros
                right = images[j] if j == 2 * pair + 1 else zeros
                rows.append(jnp.concatenate([left, right], axis=1))
            both = jnp.concatenate(rows, axis=0)
            y = jnp.dot(row_kernel, both, preferred_element_type=F32).astype(BF16)
            for j in range(2):
                at = (quad * 4 + pair * 2 + j) * PR
                for b in range(NB):
                    y_ref[at : at + PR, b * PW : (b + 1) * PW] = y[
                        b * PR : (b + 1) * PR, j * PW : (j + 1) * PW
                    ]
    matched = jnp.dot(y_ref[...], g_ref[...], preferred_element_type=F32).astype(BF16)
    matched_ref[pl.ds(first, GROUP)] = matched.reshape(GROUP, PR, PW)


def exchange_kernel(
    kind_s, coef_s, dest_ref, off_ref, weight_ref, col_ref, row_ref, pieces_ref,
    sum_ref,
    x, g_ref, r_ref, y_ref, pad_ref, padf_ref, plan_ref, plan_s, matched_ref, stage_ref,
    rb, mf, sb, rbb, sc, rc,
    x_sem, plan_sem, a_send, a_recv, b_send, b_recv, c_send, c_recv,
):
    p = lax.axis_index("patch")
    v = lax.axis_index("visit")
    c = lax.rem(p, 2)
    z = lax.rem(p // 2, SIDE)
    y = p // (2 * SIDE)
    along = jnp.where(c == 0, y, z)

    def patch_of(y_at, z_at, c_at):
        return (y_at * SIDE + z_at) * 2 + c_at

    x_copy = pltpu.make_async_copy(pieces_ref, x, x_sem)
    x_copy.start()

    barrier = pltpu.get_barrier_semaphore()

    def greet(target):
        pl.semaphore_signal(barrier, inc=1, device_id={"patch": target}, device_id_type=MESH)

    @pl.loop(1, SIDE)
    def _(i):
        for core in range(2):
            greet(patch_of(y, lax.rem(z + i, SIDE), core))
            greet(patch_of(lax.rem(y + i, SIDE), z, core))

    greet(patch_of(y, z, 1 - c))

    @pl.loop(1, VISITS)
    def _(i):
        pl.semaphore_signal(
            barrier, inc=1, device_id={"visit": lax.rem(v + i, VISITS)}, device_id_type=MESH
        )

    plan(y, z, dest_ref, off_ref, weight_ref, plan_ref, padf_ref, stage_ref)
    plan_copy = pltpu.make_async_copy(plan_ref, plan_s, plan_sem)
    plan_copy.start()
    tables(col_ref, row_ref, pad_ref, g_ref, r_ref)
    matched_ref[PIECES:, :, :] = jnp.zeros((8, PR, PW), BF16)
    plan_copy.wait()
    x_copy.wait()

    pl.semaphore_wait(barrier, 4 * (SIDE - 1) + 1 + VISITS - 1)

    def part_of(ref, at, part):
        if part == 0:
            return ref.at[at, pl.ds(0, META + CHUNK_DESTS * 64)]
        return ref.at[at, pl.ds(META + part * CHUNK_DESTS * 64, CHUNK_DESTS * 64)]

    def a_copy(message, part, slot, target):
        return pltpu.make_async_remote_copy(
            src_ref=part_of(stage_ref, message, part), dst_ref=part_of(rb, slot, part),
            send_sem=a_send.at[part, message], recv_sem=a_recv.at[part, slot],
            device_id={"patch": target}, device_id_type=MESH,
        )

    z_slot = z * 2 + c
    y_slot = y * 2 + c
    partner = patch_of(y, z, 1 - c)
    here = 2 * (SIDE - 1) + c

    def fill(message):
        for s in range(SLOTS):
            r = plan_s[1 + message // 8, (message % 8) * SLOTS + s]
            stage_ref[message, META + s * PR : META + (s + 1) * PR, :] = matched_ref[r]

    def send(message, part):
        even = lax.rem(message, 2) == 0
        distance = chosen(message // 2, ORDER)
        target = jnp.where(
            even,
            patch_of(y, lax.rem(z + distance, SIDE), 0),
            patch_of(lax.rem(y + distance, SIDE), z, 1),
        )
        slot = jnp.where(even, z_slot, y_slot)

        @pl.when(message != here)
        def _():
            a_copy(message, part, slot, target).start()

        @pl.when(message == here)
        def _():
            pltpu.make_async_copy(
                part_of(stage_ref, message, part), part_of(rb, slot, part), a_recv.at[part, slot]
            ).start()

    groups = PIECES // GROUP

    @pl.loop(0, groups)
    def _(group):
        match_group(group, kind_s, coef_s, plan_s, x, r_ref, g_ref, y_ref, matched_ref)
        fill(group)
        for part in range(CHUNKS):
            send(group, part)

    @pl.loop(groups, 16)
    def _(message):
        fill(message)
        send(message, 0)

    for part in range(1, CHUNKS):

        @pl.loop(groups, 16)
        def _(message):
            send(message, part)

    row_f = iota((PH, PW), 0).astype(F32)
    low = iota((1, PW), 1) < 64
    eye = iota((PW, PW), 0) == iota((PW, PW), 1)
    tile_row = iota((16, PW), 0)
    ones = jnp.ones((4 * 64, PW), BF16)

    def b_copy(j):
        return pltpu.make_async_remote_copy(
            src_ref=sb.at[j], dst_ref=rbb.at[along],
            send_sem=b_send.at[j], recv_sem=b_recv.at[along],
            device_id={"patch": jnp.where(c == 0, patch_of(j, z, 0), patch_of(y, j, 1))},
            device_id_type=MESH,
        )

    for part in range(CHUNKS):

        @pl.loop(0, 16)
        def _(s):
            a_copy(s, part, s, partner).wait_recv()

        if part == 0:
            mf[...] = rb[:, 0:META, :].astype(F32)

        @pl.loop(part * CHUNK_DESTS, (part + 1) * CHUNK_DESTS)
        def _(j):
            total = jnp.zeros((PH, 2 * PW), F32)
            for four in range(4):
                places = []
                blocks = []
                for pair in range(2):
                    s = four * 4 + pair * 2
                    t = jnp.where(low, mf[s, pl.ds(j, 1), :], mf[s + 1, pl.ds(j, 1), :])
                    w = jnp.where(low, mf[s, pl.ds(8 + j, 1), :], mf[s + 1, pl.ds(8 + j, 1), :])
                    places.append(jnp.where(row_f == t, w, 0.0).astype(BF16))
                    for k in range(2):
                        blocks.append(rb[s + k, pl.ds(pl.multiple_of(META + 64 * j, 16), 64), :])
                place = jnp.concatenate(places, axis=1)
                block = jnp.concatenate([jnp.concatenate(blocks, axis=0), ones], axis=1)
                total = total + jnp.dot(place, block, preferred_element_type=F32)
            sb[j, 0:PH, :] = total[:, 0:PW].astype(BF16)
            d0 = jnp.sum(jnp.where(eye, total[0:PW, PW:], 0.0), axis=0, keepdims=True)
            d1 = jnp.sum(jnp.where(eye, total[PW:, PW:], 0.0), axis=0, keepdims=True)
            h0 = d0.astype(BF16).astype(F32)
            h1 = d1.astype(BF16).astype(F32)
            tile = jnp.where(tile_row == 0, h0, jnp.where(tile_row == 1, h1, 0.0))
            tile = jnp.where(tile_row == 8, d0 - h0, jnp.where(tile_row == 9, d1 - h1, tile))
            sb[j, PH : PH + 16, :] = tile.astype(BF16)

            @pl.when(j == along)
            def _():
                pltpu.make_async_copy(sb.at[j], rbb.at[along], b_recv.at[along]).start()

            @pl.when(j != along)
            def _():
                b_copy(j).start()

    num = jnp.zeros((PH, PW), F32)
    den = jnp.zeros((8, PW), F32)
    for i in range(SIDE):
        pltpu.make_async_copy(rbb.at[i], rbb.at[i], b_recv.at[i]).wait()
        num = num + rbb[i, 0:PH, :].astype(F32)
        tile = rbb[i, PH : PH + 16, :].astype(F32)
        den = den + (tile[0:8] + tile[8:16])

    edge = jnp.zeros((HALO, PW), F32)
    for at in range(VISITS):
        start = at * STRIP - HALO
        stop = start + SPAN
        if at == 0:
            strip = jnp.concatenate([edge, num[0:stop]], axis=0)
        elif at == VISITS - 1:
            strip = jnp.concatenate([num[start:PH], edge], axis=0)
        else:
            strip = num[start:stop]
        sc[at, 0:SPAN, :] = strip
        sc[at, SPAN:, :] = den

    def c_copy(at):
        return pltpu.make_async_remote_copy(
            src_ref=sc.at[at], dst_ref=rc.at[v], send_sem=c_send.at[at], recv_sem=c_recv.at[v],
            device_id={"visit": at}, device_id_type=MESH,
        )

    @pl.loop(1, VISITS)
    def _(i):
        c_copy(lax.rem(v + i, VISITS)).start()

    pltpu.make_async_copy(sc.at[v], rc.at[v], c_recv.at[v]).start()

    for part in range(CHUNKS):

        @pl.loop(0, 16)
        def _(message):
            @pl.when(message != here)
            def _():
                a_copy(message, part, z_slot, partner).wait_send()

    @pl.loop(0, SIDE)
    def _(j):
        @pl.when(j != along)
        def _():
            b_copy(j).wait_send()

    total = jnp.zeros((SPAN + 8, PW), F32)
    for i in range(VISITS):
        pltpu.make_async_copy(rc.at[i], rc.at[i], c_recv.at[i]).wait()
        total = total + rc[i]
    sum_ref[...] = total

    @pl.loop(1, VISITS)
    def _(i):
        c_copy(lax.rem(v + i, VISITS)).wait_send()


def filter_kernel(sum_ref, taps_ref, coadd_ref, detection_ref, den_ref, pad_ref):
    v = lax.axis_index("visit")
    half = TD // 2
    pad_ref[...] = jnp.zeros_like(pad_ref)
    pad_ref[0:2, 6 : 6 + TD] = taps_ref[...].astype(F32)
    square = (PW, PW)
    lane, row = iota(square, 1), iota(square, 0)
    taps = jnp.broadcast_to(pad_ref[1:2, :], square)
    cols = pltpu.roll(taps, PW - half - 6, 1, stride=1, stride_axis=0)
    cols = jnp.where(jnp.abs(lane - row) <= half, cols, 0.0).astype(BF16)
    taps = jnp.broadcast_to(pad_ref[0:1, :], (STRIP, PW))
    rows = pltpu.roll(taps, HALO - half - 6, 1, stride=1, stride_axis=0).astype(BF16)
    den_ref[...] = jnp.zeros_like(den_ref)
    for a in range(2):
        column = jnp.broadcast_to(sum_ref[SPAN + a : SPAN + a + 1, :], square).T
        den_ref[HALO + a * PW : HALO + (a + 1) * PW, :] = column
    den = den_ref[pl.ds(pl.multiple_of(v * STRIP, STRIP), SPAN), :]
    coadd = sum_ref[0:SPAN, :] / (1.0 + den)
    coadd_ref[...] = coadd[HALO : HALO + STRIP]
    smoothed = jnp.dot(coadd.astype(BF16), cols, preferred_element_type=F32).astype(BF16)
    smoothed = jnp.concatenate([smoothed, jnp.zeros((PW - SPAN, PW), BF16)], axis=0)
    detection_ref[...] = jnp.dot(rows, smoothed, preferred_element_type=F32)


SMEM = pl.BlockSpec(memory_space=pltpu.SMEM)
VMEM = pl.BlockSpec(memory_space=pltpu.VMEM)


def exchange(pieces, dest, offsets, kernel_index, weights, basis_col, basis_row, coef_table):
    dma = pltpu.SemaphoreType.DMA
    row = (1, PIECES)
    return pl.pallas_call(
        exchange_kernel,
        out_shape=jax.ShapeDtypeStruct((SPAN + 8, PW), F32),
        in_specs=[SMEM] * 2 + [VMEM] * 5 + [pl.BlockSpec(memory_space=pl.ANY)],
        out_specs=VMEM,
        scratch_shapes=[
            pltpu.VMEM((PIECES, PR, PW), BF16),
            pltpu.VMEM((NB * PW, PW), BF16),
            pltpu.VMEM((NB, 4, 8, PW), F32),
            pltpu.VMEM((GROUP * PR, NB * PW), BF16),
            pltpu.VMEM((32, PW), F32),
            pltpu.VMEM((8, PW), F32),
            pltpu.VMEM((8, PW), I32),
            pltpu.SMEM((8, PW), I32),
            pltpu.VMEM((PIECES + 8, PR, PW), BF16),
            pltpu.VMEM((16, ROWS, PW), BF16),
            pltpu.VMEM((16, ROWS, PW), BF16),
            pltpu.VMEM((16, META, PW), F32),
            pltpu.VMEM((SIDE, PH + 16, PW), BF16),
            pltpu.VMEM((SIDE, PH + 16, PW), BF16),
            pltpu.VMEM((VISITS, SPAN + 8, PW), F32),
            pltpu.VMEM((VISITS, SPAN + 8, PW), F32),
            dma(()),
            dma(()),
            dma((CHUNKS, 16)),
            dma((CHUNKS, 16)),
            dma((SIDE,)),
            dma((SIDE,)),
            dma((VISITS,)),
            dma((VISITS,)),
        ],
        compiler_params=pltpu.CompilerParams(collective_id=0, has_side_effects=True),
        name="exchange",
    )(
        kernel_index, coef_table.T, dest.reshape(row), offsets.reshape(row), weights.reshape(row),
        basis_col, basis_row, pieces,
    )


def finish(sums, det_taps):
    out = jax.ShapeDtypeStruct((STRIP, PW), F32)
    return pl.pallas_call(
        filter_kernel,
        out_shape=(out, out),
        in_specs=[VMEM, VMEM],
        out_specs=(VMEM, VMEM),
        scratch_shapes=[pltpu.VMEM((PH + 2 * HALO, PW), F32), pltpu.VMEM((8, PW), F32)],
        name="finish",
    )(sums, det_taps)


def shards(
    pieces, dest, offsets, kernel_index, weights, basis_col, basis_row, coef_table, det_taps
):
    sums = exchange(
        pieces, dest, offsets, kernel_index, weights, basis_col, basis_row, coef_table
    )
    return finish(sums, det_taps)


def solution(mesh):
    split = P(("patch", "visit"))
    in_specs = (
        P(("patch", "visit"), None, None),
        P(("patch", "visit"), None),
        split,
        split,
        split,
        P(),
        P(),
        P(),
        P(),
    )
    out_specs = (P(("patch", "visit"), None), P(("patch", "visit"), None))
    return jax.shard_map(shards, mesh=mesh, in_specs=in_specs, out_specs=out_specs, check_vma=False)
```

time: 77.4 us -> 60.2 us (0.78)
  the two profiles are of different devices: /device:TPU:184 before, /device:TPU:56 now
where the time goes in v2:
time: 60.2 us; the launch traced here: 59.8 us
  Pallas kernels  59.2 us (98%)
  between operations  0.64 us (1%)
    pallas_call x1, Pallas kernels, exchange(): pl.pallas_call(exchange_kernel, out_shape=jax.ShapeDtypeStruct((SPAN + 8,...  57.3 us
    pallas_call x1, Pallas kernels, finish(): pl.pallas_call(filter_kernel, out_shape=(out, out), in_specs=[VMEM, VMEM]...  1.91 us

profile of v2, /device:TPU:56, one launch (start us, length us, event | category | flops | bytes accessed | tf_op | source)
XLA Modules:
  0.0 59.8 jit_solution(10059318053080057116)
XLA Ops:
  0.6 57.3 %exchange.1.sum_ref = f32[104,128]{1,0:T(8,128)} custom-call(s32[96]{0:T(128)} %kind_s.1, f32[14,40]{1,0:T(8,128)} %bitcast.4, s32[1,96]{1,0:T(1,128)} %bitcast.5, s32[1,96]{1,0:T(1,128)} %bitcast.6, bf16[1,96]{1,0:T(2,128)(2,1)} %bitcast.7, bf16[14,41]{1,0:T(8,128)(2,1)} %col_ref.1, bf16[14,41]{1,0:T(8,128)(2,1)} %row_ref.1, bf16[96,32,128]{2,1,0:T(8,128)(2,1)} %pieces_ref.1), custom_call_target="tpu_custom_call" | custom-call | tf_op jit(solution)/shard_map/exchange/pallas_call | solution.py:403
  57.9 1.9 %finish.1 = (f32[64,128]{1,0:T(8,128)}, f32[64,128]{1,0:T(8,128)}) custom-call(f32[104,128]{1,0:T(8,128)} %exchange.1.sum_ref, bf16[2,21]{1,0:T(2,128)(2,1)} %taps_ref.1), custom_call_target="tpu_custom_call" | custom-call | tf_op jit(solution)/shard_map/finish/pallas_call | solution.py:444

commit v3 on v2

--- a/solution.py
+++ b/solution.py
@@ -25,12 +25,14 @@
 STRIP = PH // VISITS
 HALO = 16
 SPAN = STRIP + 2 * HALO
-SLOTS = 16
-META = 16
-ROWS = META + SLOTS * PR
-CHUNKS = 2
-CHUNK_DESTS = 8 // CHUNKS
-ORDER = (3, 5, 4, 2, 6, 1, 7, 0)
+CHUNKS = 4
+META = 8
+DATA = 4 * PR
+ROWS = DATA + META
+DENSE = PH + 16
+ORDER = (3, 2, 5, 4, 6, 1, 7, 0)
+FAR = (3, 5, 4)
+NEAR = (2, 6, 1, 7, 0)
 
 
 def iota(shape, axis):
@@ -92,21 +94,26 @@
         plan_ref[1 + a : 2 + a, :] = PIECES + jnp.sum(
             jnp.where(pos_t == lane + a * PW, rank_t - PIECES, 0), axis=0, keepdims=True
         )
+    shape = (16 * CHUNKS * META, PW)
+    line = iota(shape, 0)
+    wanted = ((line // META) * 2 + (line & 1)) * 2
+    spots = jnp.broadcast_to(position, shape)
+    hot = jnp.concatenate(
+        [jnp.where(spots == wanted + k, 1.0, 0.0).astype(BF16) for k in range(2)], axis=1
+    )
     which = (lane // PR) & 1
-    hot = jnp.concatenate(
-        [jnp.where(pos == 2 * row + k, 1.0, 0.0).astype(BF16) for k in range(2)], axis=1
-    )
-    found = []
+    values = []
     for at in range(2):
         value = jnp.broadcast_to(padf_ref[at : at + 1, :], square).T
-        value = jnp.concatenate(
-            [jnp.where(which == k, value, 0.0).astype(BF16) for k in range(2)], axis=0
-        )
-        found.append(jnp.dot(hot, value, preferred_element_type=F32))
-    target = found[0] + (lane & (PR - 1)).astype(F32)
-    stage_ref[:, 0:META, :] = jnp.concatenate(
-        [target.reshape(16, 8, PW), found[1].reshape(16, 8, PW)], axis=1
-    ).astype(BF16)
+        values.append(
+            jnp.concatenate(
+                [jnp.where(which == k, value, 0.0).astype(BF16) for k in range(2)], axis=0
+            )
+        )
+    found = jnp.dot(hot, jnp.concatenate(values, axis=1), preferred_element_type=F32)
+    target = found[:, 0:PW] + (iota(shape, 1) & (PR - 1)).astype(F32)
+    both = jnp.where((line & 4) == 0, target, found[:, PW:])
+    stage_ref[:, :, DATA:, :] = both.reshape(16, CHUNKS, META, PW).astype(BF16)
 
 
 def match_group(group, kind_s, coef_s, plan_s, x, r_ref, g_ref, y_ref, matched_ref):
@@ -148,8 +155,8 @@
     kind_s, coef_s, dest_ref, off_ref, weight_ref, col_ref, row_ref, pieces_ref,
     sum_ref,
     x, g_ref, r_ref, y_ref, pad_ref, padf_ref, plan_ref, plan_s, matched_ref, stage_ref,
-    rb, mf, sb, rbb, sc, rc,
-    x_sem, plan_sem, a_send, a_recv, b_send, b_recv, c_send, c_recv,
+    rb, rf, mf, fd, rd, sb, rbb, sc, rc,
+    x_sem, plan_sem, a_send, a_recv, f_recv, d_send, d_recv, b_send, b_recv, c_send, c_recv,
 ):
     p = lax.axis_index("patch")
     v = lax.axis_index("visit")
@@ -179,9 +186,12 @@
 
     @pl.loop(1, VISITS)
     def _(i):
-        pl.semaphore_signal(
-            barrier, inc=1, device_id={"visit": lax.rem(v + i, VISITS)}, device_id_type=MESH
-        )
+        for core in range(2):
+            pl.semaphore_signal(
+                barrier, inc=1,
+                device_id={"patch": patch_of(y, z, core), "visit": lax.rem(v + i, VISITS)},
+                device_id_type=MESH,
+            )
 
     plan(y, z, dest_ref, off_ref, weight_ref, plan_ref, padf_ref, stage_ref)
     plan_copy = pltpu.make_async_copy(plan_ref, plan_s, plan_sem)
@@ -191,49 +201,126 @@
     plan_copy.wait()
     x_copy.wait()
 
-    pl.semaphore_wait(barrier, 4 * (SIDE - 1) + 1 + VISITS - 1)
-
-    def part_of(ref, at, part):
-        if part == 0:
-            return ref.at[at, pl.ds(0, META + CHUNK_DESTS * 64)]
-        return ref.at[at, pl.ds(META + part * CHUNK_DESTS * 64, CHUNK_DESTS * 64)]
-
-    def a_copy(message, part, slot, target):
+    pl.semaphore_wait(barrier, 4 * (SIDE - 1) + 1 + 2 * (VISITS - 1))
+
+    partner = patch_of(y, z, 1 - c)
+
+    def near_copy(message, part, slot, target):
         return pltpu.make_async_remote_copy(
-            src_ref=part_of(stage_ref, message, part), dst_ref=part_of(rb, slot, part),
-            send_sem=a_send.at[part, message], recv_sem=a_recv.at[part, slot],
+            src_ref=stage_ref.at[message, part], dst_ref=rb.at[slot, part],
+            send_sem=a_send.at[message, part], recv_sem=a_recv.at[slot, part],
             device_id={"patch": target}, device_id_type=MESH,
         )
 
-    z_slot = z * 2 + c
-    y_slot = y * 2 + c
-    partner = patch_of(y, z, 1 - c)
-    here = 2 * (SIDE - 1) + c
+    def far_copy(message, part, index, target):
+        slot = v * 2 + c
+        return pltpu.make_async_remote_copy(
+            src_ref=stage_ref.at[message, part], dst_ref=rf.at[index, slot],
+            send_sem=a_send.at[message, part], recv_sem=f_recv.at[index, slot],
+            device_id={"patch": target, "visit": part}, device_id_type=MESH,
+        )
 
     def fill(message):
-        for s in range(SLOTS):
-            r = plan_s[1 + message // 8, (message % 8) * SLOTS + s]
-            stage_ref[message, META + s * PR : META + (s + 1) * PR, :] = matched_ref[r]
-
-    def send(message, part):
-        even = lax.rem(message, 2) == 0
-        distance = chosen(message // 2, ORDER)
+        for s in range(16):
+            r = plan_s[1 + message // 8, (message % 8) * 16 + s]
+            stage_ref[message, s // 4, (s % 4) * PR : (s % 4 + 1) * PR, :] = matched_ref[r]
+
+    def turn_part(turn):
+        return lax.rem(v + 1 + turn, VISITS)
+
+    def send_near(message, part):
+        turn = message // 2
+        core = lax.rem(message, 2)
+        distance = chosen(turn, ORDER)
+        slot = chosen(turn, tuple(max(0, NEAR.index(o) if o in NEAR else 0) for o in ORDER)) * 2 + c
         target = jnp.where(
-            even,
+            core == 0,
             patch_of(y, lax.rem(z + distance, SIDE), 0),
             patch_of(lax.rem(y + distance, SIDE), z, 1),
         )
-        slot = jnp.where(even, z_slot, y_slot)
-
-        @pl.when(message != here)
+        here = (distance == 0) & (core == c)
+
+        @pl.when(jnp.logical_not(here))
         def _():
-            a_copy(message, part, slot, target).start()
-
-        @pl.when(message == here)
+            near_copy(message, part, slot, target).start()
+
+        @pl.when(here)
         def _():
             pltpu.make_async_copy(
-                part_of(stage_ref, message, part), part_of(rb, slot, part), a_recv.at[part, slot]
+                stage_ref.at[message, part], rb.at[slot, part], a_recv.at[slot, part]
             ).start()
+
+    def send_far(message, part):
+        core = lax.rem(message, 2)
+        index = chosen(message // 2, tuple(FAR.index(o) if o in FAR else 0 for o in ORDER))
+        here = (part == v) & (core == c)
+
+        @pl.when(jnp.logical_not(here))
+        def _():
+            far_copy(message, part, index, patch_of(y, z, core)).start()
+
+        @pl.when(here)
+        def _():
+            slot = v * 2 + c
+            pltpu.make_async_copy(
+                stage_ref.at[message, part], rf.at[index, slot], f_recv.at[index, slot]
+            ).start()
+
+    row_f = iota((PH, PW), 0).astype(F32)
+    low = iota((1, PW), 1) < 64
+    eye = iota((PW, PW), 0) == iota((PW, PW), 1)
+    tile_row = iota((16, PW), 0)
+
+    def add_up(count, e, load):
+        places = []
+        blocks = []
+        for s in range(0, count, 2):
+            t = jnp.where(low, mf[s, pl.ds(e, 1), :], mf[s + 1, pl.ds(e, 1), :])
+            w = jnp.where(low, mf[s, pl.ds(4 + e, 1), :], mf[s + 1, pl.ds(4 + e, 1), :])
+            places.append(jnp.where(row_f == t, w, 0.0).astype(BF16))
+            for k in range(2):
+                blocks.append(load(s + k, pl.ds(pl.multiple_of(64 * e, 64), 64)))
+        place = jnp.concatenate(places, axis=1)
+        ones = jnp.ones((64 * count, PW), BF16)
+        block = jnp.concatenate([jnp.concatenate(blocks, axis=0), ones], axis=1)
+        total = jnp.dot(place, block, preferred_element_type=F32)
+        d0 = jnp.sum(jnp.where(eye, total[0:PW, PW:], 0.0), axis=0, keepdims=True)
+        d1 = jnp.sum(jnp.where(eye, total[PW:, PW:], 0.0), axis=0, keepdims=True)
+        den = jnp.where(tile_row == 0, d0, jnp.where(tile_row == 1, d1, 0.0))
+        return total[:, 0:PW], den[0:8]
+
+    def dense(ref, lead, total, den):
+        high = den.astype(BF16).astype(F32)
+        ref[lead + (slice(0, PH), slice(None))] = total.astype(BF16)
+        ref[lead + (slice(PH, DENSE), slice(None))] = jnp.concatenate(
+            [high, den - high], axis=0
+        ).astype(BF16)
+
+    def dense_copy(index, e):
+        distance = FAR[index]
+        target = jnp.where(
+            c == 0,
+            patch_of(y, lax.rem(z + distance, SIDE), 0),
+            patch_of(lax.rem(y + distance, SIDE), z, 1),
+        )
+        return pltpu.make_async_remote_copy(
+            src_ref=fd.at[index, e], dst_ref=rd.at[index, e],
+            send_sem=d_send.at[index, e], recv_sem=d_recv.at[index, e],
+            device_id={"patch": target}, device_id_type=MESH,
+        )
+
+    def add_far(index):
+        @pl.loop(0, 2 * VISITS)
+        def _(s):
+            pltpu.make_async_copy(rf.at[index, s], rf.at[index, s], f_recv.at[index, s]).wait()
+
+        mf[0 : 2 * VISITS] = rf[index, :, DATA:, :].astype(F32)
+
+        @pl.loop(0, 2)
+        def _(e):
+            total, den = add_up(2 * VISITS, e, lambda s, rows: rf[index, s, rows, :])
+            dense(fd, (index, e), total, den)
+            dense_copy(index, e).start()
 
     groups = PIECES // GROUP
 
@@ -241,25 +328,43 @@
     def _(group):
         match_group(group, kind_s, coef_s, plan_s, x, r_ref, g_ref, y_ref, matched_ref)
         fill(group)
-        for part in range(CHUNKS):
-            send(group, part)
-
-    @pl.loop(groups, 16)
+        near = group // 2 == 1
+
+        @pl.loop(0, CHUNKS)
+        def _(turn):
+            @pl.when(near)
+            def _():
+                send_near(group, turn_part(turn))
+
+            @pl.when(jnp.logical_not(near))
+            def _():
+                send_far(group, turn_part(turn))
+
+        @pl.when(group == 3)
+        def _():
+            add_far(0)
+
+    @pl.loop(groups, groups + 2)
     def _(message):
         fill(message)
-        send(message, 0)
-
-    for part in range(1, CHUNKS):
-
-        @pl.loop(groups, 16)
+
+        @pl.loop(0, CHUNKS)
+        def _(turn):
+            send_far(message, turn_part(turn))
+
+    @pl.loop(groups + 2, 16)
+    def _(message):
+        fill(message)
+        send_near(message, turn_part(0))
+
+    @pl.loop(1, CHUNKS)
+    def _(turn):
+        @pl.loop(groups + 2, 16)
         def _(message):
-            send(message, part)
-
-    row_f = iota((PH, PW), 0).astype(F32)
-    low = iota((1, PW), 1) < 64
-    eye = iota((PW, PW), 0) == iota((PW, PW), 1)
-    tile_row = iota((16, PW), 0)
-    ones = jnp.ones((4 * 64, PW), BF16)
+            send_near(message, turn_part(turn))
+
+    add_far(1)
+    add_far(2)
 
     def b_copy(j):
         return pltpu.make_async_remote_copy(
@@ -269,39 +374,30 @@
             device_id_type=MESH,
         )
 
-    for part in range(CHUNKS):
-
-        @pl.loop(0, 16)
+    def add_near(turn):
+        part = turn_part(turn)
+
+        @pl.loop(0, 2 * len(NEAR))
         def _(s):
-            a_copy(s, part, s, partner).wait_recv()
-
-        if part == 0:
-            mf[...] = rb[:, 0:META, :].astype(F32)
-
-        @pl.loop(part * CHUNK_DESTS, (part + 1) * CHUNK_DESTS)
-        def _(j):
-            total = jnp.zeros((PH, 2 * PW), F32)
-            for four in range(4):
-                places = []
-                blocks = []
-                for pair in range(2):
-                    s = four * 4 + pair * 2
-                    t = jnp.where(low, mf[s, pl.ds(j, 1), :], mf[s + 1, pl.ds(j, 1), :])
-                    w = jnp.where(low, mf[s, pl.ds(8 + j, 1), :], mf[s + 1, pl.ds(8 + j, 1), :])
-                    places.append(jnp.where(row_f == t, w, 0.0).astype(BF16))
-                    for k in range(2):
-                        blocks.append(rb[s + k, pl.ds(pl.multiple_of(META + 64 * j, 16), 64), :])
-                place = jnp.concatenate(places, axis=1)
-                block = jnp.concatenate([jnp.concatenate(blocks, axis=0), ones], axis=1)
-                total = total + jnp.dot(place, block, preferred_element_type=F32)
-            sb[j, 0:PH, :] = total[:, 0:PW].astype(BF16)
-            d0 = jnp.sum(jnp.where(eye, total[0:PW, PW:], 0.0), axis=0, keepdims=True)
-            d1 = jnp.sum(jnp.where(eye, total[PW:, PW:], 0.0), axis=0, keepdims=True)
-            h0 = d0.astype(BF16).astype(F32)
-            h1 = d1.astype(BF16).astype(F32)
-            tile = jnp.where(tile_row == 0, h0, jnp.where(tile_row == 1, h1, 0.0))
-            tile = jnp.where(tile_row == 8, d0 - h0, jnp.where(tile_row == 9, d1 - h1, tile))
-            sb[j, PH : PH + 16, :] = tile.astype(BF16)
+            pltpu.make_async_copy(rb.at[s, part], rb.at[s, part], a_recv.at[s, part]).wait()
+
+        mf[...] = rb[:, part, DATA:, :].astype(F32)
+        last = turn == CHUNKS - 1
+        if last:
+            for index in range(len(FAR)):
+                for e in range(2):
+                    dense_copy(index, e).wait_recv()
+
+        @pl.loop(0, 2)
+        def _(e):
+            total, den = add_up(2 * len(NEAR), e, lambda s, rows: rb[s, part, rows, :])
+            if last:
+                for index in range(len(FAR)):
+                    total = total + rd[index, e, 0:PH, :].astype(F32)
+                    tile = rd[index, e, PH:DENSE, :].astype(F32)
+                    den = den + (tile[0:8] + tile[8:16])
+            j = part * 2 + e
+            dense(sb, (j,), total, den)
 
             @pl.when(j == along)
             def _():
@@ -310,13 +406,16 @@
             @pl.when(j != along)
             def _():
                 b_copy(j).start()
+
+    for turn in range(CHUNKS):
+        add_near(turn)
 
     num = jnp.zeros((PH, PW), F32)
     den = jnp.zeros((8, PW), F32)
     for i in range(SIDE):
         pltpu.make_async_copy(rbb.at[i], rbb.at[i], b_recv.at[i]).wait()
         num = num + rbb[i, 0:PH, :].astype(F32)
-        tile = rbb[i, PH : PH + 16, :].astype(F32)
+        tile = rbb[i, PH:DENSE, :].astype(F32)
         den = den + (tile[0:8] + tile[8:16])
 
     edge = jnp.zeros((HALO, PW), F32)
@@ -344,13 +443,23 @@
 
     pltpu.make_async_copy(sc.at[v], rc.at[v], c_recv.at[v]).start()
 
-    for part in range(CHUNKS):
-
-        @pl.loop(0, 16)
-        def _(message):
-            @pl.when(message != here)
+    @pl.loop(0, 16)
+    def _(message):
+        distance = chosen(message // 2, ORDER)
+        core = lax.rem(message, 2)
+        far = (distance >= 3) & (distance <= 5)
+
+        @pl.loop(0, CHUNKS)
+        def _(part):
+            here = (core == c) & ((far & (part == v)) | (distance == 0))
+
+            @pl.when(jnp.logical_not(here))
             def _():
-                a_copy(message, part, z_slot, partner).wait_send()
+                near_copy(message, part, 0, partner).wait_send()
+
+    for index in range(len(FAR)):
+        for e in range(2):
+            dense_copy(index, e).wait_send()
 
     @pl.loop(0, SIDE)
     def _(j):
@@ -415,17 +524,23 @@
             pltpu.VMEM((8, PW), I32),
             pltpu.SMEM((8, PW), I32),
             pltpu.VMEM((PIECES + 8, PR, PW), BF16),
-            pltpu.VMEM((16, ROWS, PW), BF16),
-            pltpu.VMEM((16, ROWS, PW), BF16),
-            pltpu.VMEM((16, META, PW), F32),
-            pltpu.VMEM((SIDE, PH + 16, PW), BF16),
-            pltpu.VMEM((SIDE, PH + 16, PW), BF16),
+            pltpu.VMEM((16, CHUNKS, ROWS, PW), BF16),
+            pltpu.VMEM((2 * len(NEAR), CHUNKS, ROWS, PW), BF16),
+            pltpu.VMEM((len(FAR), 2 * VISITS, ROWS, PW), BF16),
+            pltpu.VMEM((2 * len(NEAR), META, PW), F32),
+            pltpu.VMEM((len(FAR), 2, DENSE, PW), BF16),
+            pltpu.VMEM((len(FAR), 2, DENSE, PW), BF16),
+            pltpu.VMEM((SIDE, DENSE, PW), BF16),
+            pltpu.VMEM((SIDE, DENSE, PW), BF16),
             pltpu.VMEM((VISITS, SPAN + 8, PW), F32),
             pltpu.VMEM((VISITS, SPAN + 8, PW), F32),
             dma(()),
             dma(()),
-            dma((CHUNKS, 16)),
-            dma((CHUNKS, 16)),
+            dma((16, CHUNKS)),
+            dma((2 * len(NEAR), CHUNKS)),
+            dma((len(FAR), 2 * VISITS)),
+            dma((len(FAR), 2)),
+            dma((len(FAR), 2)),
             dma((SIDE,)),
             dma((SIDE,)),
             dma((VISITS,)),

time: 60.2 us -> 64.3 us (1.068)
  the two profiles are of different devices: /device:TPU:56 before, /device:TPU:77 now
where the time goes in v3:
time: 64.3 us; the launch traced here: 64.1 us
  Pallas kernels  63.4 us (99%)
    pallas_call x1, Pallas kernels, exchange(): pl.pallas_call(exchange_kernel, out_shape=jax.ShapeDtypeStruct((SPAN + 8,...  61.5 us
    pallas_call x1, Pallas kernels, finish(): pl.pallas_call(filter_kernel, out_shape=(out, out), in_specs=[VMEM, VMEM]...  1.91 us

profile of v3, /device:TPU:77, one launch (start us, length us, event | category | flops | bytes accessed | tf_op | source)
XLA Modules:
  0.0 64.1 jit_solution(18000133082178105562)
XLA Ops:
  0.6 61.5 %exchange.1.sum_ref = f32[104,128]{1,0:T(8,128)} custom-call(s32[96]{0:T(128)} %kind_s.1, f32[14,40]{1,0:T(8,128)} %bitcast.4, s32[1,96]{1,0:T(1,128)} %bitcast.5, s32[1,96]{1,0:T(1,128)} %bitcast.6, bf16[1,96]{1,0:T(2,128)(2,1)} %bitcast.7, bf16[14,41]{1,0:T(8,128)(2,1)} %col_ref.1, bf16[14,41]{1,0:T(8,128)(2,1)} %row_ref.1, bf16[96,32,128]{2,1,0:T(8,128)(2,1)} %pieces_ref.1), custom_call_target="tpu_custom_call" | custom-call | tf_op jit(solution)/shard_map/exchange/pallas_call | solution.py:512
  62.2 1.9 %finish.1 = (f32[64,128]{1,0:T(8,128)}, f32[64,128]{1,0:T(8,128)}) custom-call(f32[104,128]{1,0:T(8,128)} %exchange.1.sum_ref, bf16[2,21]{1,0:T(2,128)(2,1)} %taps_ref.1), custom_call_target="tpu_custom_call" | custom-call | tf_op jit(solution)/shard_map/finish/pallas_call | solution.py:559

commit v4 on v2

--- a/solution.py
+++ b/solution.py
@@ -21,6 +21,7 @@
 TD = 21
 SIDE = 8
 VISITS = 4
+READY = 1
 GROUP = 16
 STRIP = PH // VISITS
 HALO = 16
@@ -28,9 +29,10 @@
 SLOTS = 16
 META = 16
 ROWS = META + SLOTS * PR
-CHUNKS = 2
+LONG = STRIP + 2 * HALO + 8
+CHUNKS = 4
 CHUNK_DESTS = 8 // CHUNKS
-ORDER = (3, 5, 4, 2, 6, 1, 7, 0)
+ORDER = (4, 3, 5, 2, 6, 1, 7, 0)
 
 
 def iota(shape, axis):
@@ -63,7 +65,7 @@
         r_ref[b] = r.reshape(4, 8, PW)
 
 
-def plan(y, z, dest_ref, off_ref, weight_ref, plan_ref, padf_ref, stage_ref):
+def plan(y, z, c, dest_ref, off_ref, weight_ref, plan_ref, padf_ref, stage_ref):
     plan_ref[...] = jnp.full_like(plan_ref, -1)
     plan_ref[0:1, 0:PIECES] = dest_ref[...]
     padf_ref[...] = jnp.zeros_like(padf_ref)
@@ -76,7 +78,8 @@
     earlier = jnp.sum(jnp.where((d == d_t) & (row < lane), 1, 0), axis=0, keepdims=True)
     d1 = plan_ref[0:1, :]
     y_to, z_to, c_to = d1 >> 4, (d1 >> 1) & 7, d1 & 1
-    distance = jnp.where(c_to == 0, z_to - z, y_to - y) & 7
+    distance = jnp.where(c_to == 0, z_to - z, y_to - y)
+    distance = jnp.where(c_to == c, distance, -distance) & 7
     inner = jnp.where(c_to == 0, y_to, z_to)
     turn = chosen(distance, tuple(ORDER.index(o) for o in range(SIDE)))
     position = ((turn * 2 + c_to) * 8 + inner) * 2 + earlier
@@ -145,11 +148,11 @@
 
 
 def exchange_kernel(
-    kind_s, coef_s, dest_ref, off_ref, weight_ref, col_ref, row_ref, pieces_ref,
+    kind_in, coef_in, dest_in, off_in, weight_in, col_in, row_in, pieces_ref,
     sum_ref,
-    x, g_ref, r_ref, y_ref, pad_ref, padf_ref, plan_ref, plan_s, matched_ref, stage_ref,
+    kind_s, coef_s, dest_ref, off_ref, weight_ref, col_ref, row_ref, x, g_ref, r_ref, y_ref, pad_ref, padf_ref, plan_ref, plan_s, matched_ref, stage_ref,
     rb, mf, sb, rbb, sc, rc,
-    x_sem, plan_sem, a_send, a_recv, b_send, b_recv, c_send, c_recv,
+    in_sem, x_sem, plan_sem, a_send, a_recv, b_send, b_recv, c_send, c_recv,
 ):
     p = lax.axis_index("patch")
     v = lax.axis_index("visit")
@@ -161,6 +164,17 @@
     def patch_of(y_at, z_at, c_at):
         return (y_at * SIDE + z_at) * 2 + c_at
 
+    small = [
+        pltpu.make_async_copy(source, target, in_sem.at[at])
+        for at, (source, target) in enumerate(
+            (
+                (dest_in, dest_ref), (off_in, off_ref), (weight_in, weight_ref),
+                (col_in, col_ref), (row_in, row_ref), (kind_in, kind_s), (coef_in, coef_s),
+            )
+        )
+    ]
+    for copy in small:
+        copy.start()
     x_copy = pltpu.make_async_copy(pieces_ref, x, x_sem)
     x_copy.start()
 
@@ -183,7 +197,9 @@
             barrier, inc=1, device_id={"visit": lax.rem(v + i, VISITS)}, device_id_type=MESH
         )
 
-    plan(y, z, dest_ref, off_ref, weight_ref, plan_ref, padf_ref, stage_ref)
+    for copy in small:
+        copy.wait()
+    plan(y, z, c, dest_ref, off_ref, weight_ref, plan_ref, padf_ref, stage_ref)
     plan_copy = pltpu.make_async_copy(plan_ref, plan_s, plan_sem)
     plan_copy.start()
     tables(col_ref, row_ref, pad_ref, g_ref, r_ref)
@@ -191,8 +207,6 @@
     plan_copy.wait()
     x_copy.wait()
 
-    pl.semaphore_wait(barrier, 4 * (SIDE - 1) + 1 + VISITS - 1)
-
     def part_of(ref, at, part):
         if part == 0:
             return ref.at[at, pl.ds(0, META + CHUNK_DESTS * 64)]
@@ -218,6 +232,7 @@
     def send(message, part):
         even = lax.rem(message, 2) == 0
         distance = chosen(message // 2, ORDER)
+        distance = jnp.where(lax.rem(message, 2) == c, distance, lax.rem(SIDE - distance, SIDE))
         target = jnp.where(
             even,
             patch_of(y, lax.rem(z + distance, SIDE), 0),
@@ -235,42 +250,78 @@
                 part_of(stage_ref, message, part), part_of(rb, slot, part), a_recv.at[part, slot]
             ).start()
 
+    def send_fixed(message, part):
+        core = message % 2
+        distance = ORDER[message // 2]
+        step = jnp.where(c == core, distance, (SIDE - distance) % SIDE)
+        if core == 0:
+            target, slot = patch_of(y, lax.rem(z + step, SIDE), 0), z_slot
+        else:
+            target, slot = patch_of(lax.rem(y + step, SIDE), z, 1), y_slot
+        if distance:
+            a_copy(message, part, slot, target).start()
+        else:
+
+            @pl.when(c != core)
+            def _():
+                a_copy(message, part, slot, target).start()
+
+            @pl.when(c == core)
+            def _():
+                pltpu.make_async_copy(
+                    part_of(stage_ref, message, part), part_of(rb, slot, part),
+                    a_recv.at[part, slot],
+                ).start()
+
     groups = PIECES // GROUP
 
     @pl.loop(0, groups)
     def _(group):
         match_group(group, kind_s, coef_s, plan_s, x, r_ref, g_ref, y_ref, matched_ref)
         fill(group)
-        for part in range(CHUNKS):
-            send(group, part)
-
-    @pl.loop(groups, 16)
-    def _(message):
-        fill(message)
-        send(message, 0)
-
-    for part in range(1, CHUNKS):
-
-        @pl.loop(groups, 16)
-        def _(message):
-            send(message, part)
+
+        @pl.when(group == READY)
+        def _():
+            pl.semaphore_wait(barrier, 4 * (SIDE - 1) + 1 + VISITS - 1)
+
+            @pl.loop(0, READY)
+            def _(message):
+                for part in range(CHUNKS):
+                    send(message, part)
+
+        @pl.when(group >= READY)
+        def _():
+            for part in range(CHUNKS):
+                send(group, part)
+
+    for part in range(CHUNKS):
+        for message in range(groups, 16):
+            if part == 0:
+                fill(message)
+            send_fixed(message, part)
 
     row_f = iota((PH, PW), 0).astype(F32)
     low = iota((1, PW), 1) < 64
     eye = iota((PW, PW), 0) == iota((PW, PW), 1)
-    tile_row = iota((16, PW), 0)
+    tile_row = iota((8, PW), 0)
     ones = jnp.ones((4 * 64, PW), BF16)
-
-    def b_copy(j):
+    edge = jnp.zeros((HALO, PW), F32)
+
+    def split(den):
+        high = den.astype(BF16).astype(F32)
+        return jnp.where(tile_row < 4, high, pltpu.roll(den - high, 4, 0))
+
+    def joined(tile):
+        return tile + pltpu.roll(tile, 4, 0)
+
+    def b_copy(part, at):
         return pltpu.make_async_remote_copy(
-            src_ref=sb.at[j], dst_ref=rbb.at[along],
-            send_sem=b_send.at[j], recv_sem=b_recv.at[along],
-            device_id={"patch": jnp.where(c == 0, patch_of(j, z, 0), patch_of(y, j, 1))},
-            device_id_type=MESH,
-        )
-
-    for part in range(CHUNKS):
-
+            src_ref=sb.at[part, at], dst_ref=rbb.at[v, part],
+            send_sem=b_send.at[part, at], recv_sem=b_recv.at[part, v],
+            device_id={"visit": at}, device_id_type=MESH,
+        )
+
+    def add_up(part):
         @pl.loop(0, 16)
         def _(s):
             a_copy(s, part, s, partner).wait_recv()
@@ -278,8 +329,9 @@
         if part == 0:
             mf[...] = rb[:, 0:META, :].astype(F32)
 
-        @pl.loop(part * CHUNK_DESTS, (part + 1) * CHUNK_DESTS)
-        def _(j):
+        @pl.loop(0, CHUNK_DESTS)
+        def _(e):
+            j = part * CHUNK_DESTS + e
             total = jnp.zeros((PH, 2 * PW), F32)
             for four in range(4):
                 places = []
@@ -294,55 +346,61 @@
                 place = jnp.concatenate(places, axis=1)
                 block = jnp.concatenate([jnp.concatenate(blocks, axis=0), ones], axis=1)
                 total = total + jnp.dot(place, block, preferred_element_type=F32)
-            sb[j, 0:PH, :] = total[:, 0:PW].astype(BF16)
             d0 = jnp.sum(jnp.where(eye, total[0:PW, PW:], 0.0), axis=0, keepdims=True)
             d1 = jnp.sum(jnp.where(eye, total[PW:, PW:], 0.0), axis=0, keepdims=True)
-            h0 = d0.astype(BF16).astype(F32)
-            h1 = d1.astype(BF16).astype(F32)
-            tile = jnp.where(tile_row == 0, h0, jnp.where(tile_row == 1, h1, 0.0))
-            tile = jnp.where(tile_row == 8, d0 - h0, jnp.where(tile_row == 9, d1 - h1, tile))
-            sb[j, PH : PH + 16, :] = tile.astype(BF16)
+            den = jnp.where(tile_row == 0, d0, jnp.where(tile_row == 1, d1, 0.0))
+            tile = split(den).astype(BF16)
+            for at in range(VISITS):
+                start = at * STRIP - HALO
+                stop = start + SPAN
+                if at == 0:
+                    strip = jnp.concatenate([edge, total[0:stop, 0:PW]], axis=0)
+                elif at == VISITS - 1:
+                    strip = jnp.concatenate([total[start:PH, 0:PW], edge], axis=0)
+                else:
+                    strip = total[start:stop, 0:PW]
+                sb[part, at, e, 0:SPAN, :] = strip.astype(BF16)
+                sb[part, at, e, SPAN:, :] = tile
+
+        @pl.loop(1, VISITS)
+        def _(i):
+            b_copy(part, lax.rem(v + i, VISITS)).start()
+
+        pltpu.make_async_copy(sb.at[part, v], rbb.at[v, part], b_recv.at[part, v]).start()
+
+    def c_copy(j):
+        return pltpu.make_async_remote_copy(
+            src_ref=sc.at[j], dst_ref=rc.at[along],
+            send_sem=c_send.at[j], recv_sem=c_recv.at[along],
+            device_id={"patch": jnp.where(c == 0, patch_of(j, z, 0), patch_of(y, j, 1))},
+            device_id_type=MESH,
+        )
+
+    def collect(part):
+        for at in range(VISITS):
+            pltpu.make_async_copy(rbb.at[at, part], rbb.at[at, part], b_recv.at[part, at]).wait()
+
+        for e in range(CHUNK_DESTS):
+            j = part * CHUNK_DESTS + e
+            total = rbb[0, part, e].astype(F32)
+            for at in range(1, VISITS):
+                total = total + rbb[at, part, e].astype(F32)
+            sc[j, 0:SPAN, :] = total[0:SPAN].astype(BF16)
+            sc[j, SPAN:, :] = split(joined(total[SPAN:])).astype(BF16)
 
             @pl.when(j == along)
             def _():
-                pltpu.make_async_copy(sb.at[j], rbb.at[along], b_recv.at[along]).start()
+                pltpu.make_async_copy(sc.at[j], rc.at[along], c_recv.at[along]).start()
 
             @pl.when(j != along)
             def _():
-                b_copy(j).start()
-
-    num = jnp.zeros((PH, PW), F32)
-    den = jnp.zeros((8, PW), F32)
-    for i in range(SIDE):
-        pltpu.make_async_copy(rbb.at[i], rbb.at[i], b_recv.at[i]).wait()
-        num = num + rbb[i, 0:PH, :].astype(F32)
-        tile = rbb[i, PH : PH + 16, :].astype(F32)
-        den = den + (tile[0:8] + tile[8:16])
-
-    edge = jnp.zeros((HALO, PW), F32)
-    for at in range(VISITS):
-        start = at * STRIP - HALO
-        stop = start + SPAN
-        if at == 0:
-            strip = jnp.concatenate([edge, num[0:stop]], axis=0)
-        elif at == VISITS - 1:
-            strip = jnp.concatenate([num[start:PH], edge], axis=0)
-        else:
-            strip = num[start:stop]
-        sc[at, 0:SPAN, :] = strip
-        sc[at, SPAN:, :] = den
-
-    def c_copy(at):
-        return pltpu.make_async_remote_copy(
-            src_ref=sc.at[at], dst_ref=rc.at[v], send_sem=c_send.at[at], recv_sem=c_recv.at[v],
-            device_id={"visit": at}, device_id_type=MESH,
-        )
-
-    @pl.loop(1, VISITS)
-    def _(i):
-        c_copy(lax.rem(v + i, VISITS)).start()
-
-    pltpu.make_async_copy(sc.at[v], rc.at[v], c_recv.at[v]).start()
+                c_copy(j).start()
+
+    add_up(0)
+    for part in range(1, CHUNKS):
+        add_up(part)
+        collect(part - 1)
+    collect(CHUNKS - 1)
 
     for part in range(CHUNKS):
 
@@ -352,21 +410,22 @@
             def _():
                 a_copy(message, part, z_slot, partner).wait_send()
 
+        @pl.loop(1, VISITS)
+        def _(i):
+            b_copy(part, lax.rem(v + i, VISITS)).wait_send()
+
+    total = jnp.zeros((LONG, PW), F32)
+    for i in range(SIDE):
+        pltpu.make_async_copy(rc.at[i], rc.at[i], c_recv.at[i]).wait()
+        total = total + rc[i].astype(F32)
+    sum_ref[0:SPAN, :] = total[0:SPAN]
+    sum_ref[SPAN:, :] = joined(total[SPAN:])
+
     @pl.loop(0, SIDE)
     def _(j):
         @pl.when(j != along)
         def _():
-            b_copy(j).wait_send()
-
-    total = jnp.zeros((SPAN + 8, PW), F32)
-    for i in range(VISITS):
-        pltpu.make_async_copy(rc.at[i], rc.at[i], c_recv.at[i]).wait()
-        total = total + rc[i]
-    sum_ref[...] = total
-
-    @pl.loop(1, VISITS)
-    def _(i):
-        c_copy(lax.rem(v + i, VISITS)).wait_send()
+            c_copy(j).wait_send()
 
 
 def filter_kernel(sum_ref, taps_ref, coadd_ref, detection_ref, den_ref, pad_ref):
@@ -393,7 +452,6 @@
     detection_ref[...] = jnp.dot(rows, smoothed, preferred_element_type=F32)
 
 
-SMEM = pl.BlockSpec(memory_space=pltpu.SMEM)
 VMEM = pl.BlockSpec(memory_space=pltpu.VMEM)
 
 
@@ -402,10 +460,17 @@
     row = (1, PIECES)
     return pl.pallas_call(
         exchange_kernel,
-        out_shape=jax.ShapeDtypeStruct((SPAN + 8, PW), F32),
-        in_specs=[SMEM] * 2 + [VMEM] * 5 + [pl.BlockSpec(memory_space=pl.ANY)],
+        out_shape=pltpu.VMEM((LONG, PW), F32),
+        in_specs=[pl.BlockSpec(memory_space=pl.ANY)] * 8,
         out_specs=VMEM,
         scratch_shapes=[
+            pltpu.SMEM((PIECES,), I32),
+            pltpu.SMEM(coef_table.shape[::-1], F32),
+            pltpu.VMEM(row, I32),
+            pltpu.VMEM(row, I32),
+            pltpu.VMEM(row, BF16),
+            pltpu.VMEM(basis_col.shape, BF16),
+            pltpu.VMEM(basis_row.shape, BF16),
             pltpu.VMEM((PIECES, PR, PW), BF16),
             pltpu.VMEM((NB * PW, PW), BF16),
             pltpu.VMEM((NB, 4, 8, PW), F32),
@@ -418,18 +483,19 @@
             pltpu.VMEM((16, ROWS, PW), BF16),
             pltpu.VMEM((16, ROWS, PW), BF16),
             pltpu.VMEM((16, META, PW), F32),
-            pltpu.VMEM((SIDE, PH + 16, PW), BF16),
-            pltpu.VMEM((SIDE, PH + 16, PW), BF16),
-            pltpu.VMEM((VISITS, SPAN + 8, PW), F32),
-            pltpu.VMEM((VISITS, SPAN + 8, PW), F32),
+            pltpu.VMEM((CHUNKS, VISITS, CHUNK_DESTS, LONG, PW), BF16),
+            pltpu.VMEM((VISITS, CHUNKS, CHUNK_DESTS, LONG, PW), BF16),
+            pltpu.VMEM((SIDE, LONG, PW), BF16),
+            pltpu.VMEM((SIDE, LONG, PW), BF16),
+            dma((7,)),
             dma(()),
             dma(()),
             dma((CHUNKS, 16)),
             dma((CHUNKS, 16)),
+            dma((CHUNKS, VISITS)),
+            dma((CHUNKS, VISITS)),
             dma((SIDE,)),
             dma((SIDE,)),
-            dma((VISITS,)),
-            dma((VISITS,)),
         ],
         compiler_params=pltpu.CompilerParams(collective_id=0, has_side_effects=True),
         name="exchange",
@@ -448,7 +514,7 @@
         out_specs=(VMEM, VMEM),
         scratch_shapes=[pltpu.VMEM((PH + 2 * HALO, PW), F32), pltpu.VMEM((8, PW), F32)],
         name="finish",
-    )(sums, det_taps)
+    )(pltpu.with_memory_space_constraint(sums, pltpu.VMEM), det_taps)
 
 
 def shards(

time: 60.2 us -> 57.6 us (0.957)
  Pallas kernels: 59.2 us -> 56.8 us
    pallas_call x1, Pallas kernels: 57.3 us -> 55 us  [exchange(): pl.pallas_call(exchange_kernel, out_shape=pltpu.VMEM((LONG, PW), F32), in...]
where the time goes in v4:
time: 57.6 us; the launch traced here: 57.4 us
  Pallas kernels  56.8 us (99%)
  between operations  0.64 us (1%)
    pallas_call x1, Pallas kernels, exchange(): pl.pallas_call(exchange_kernel, out_shape=pltpu.VMEM((LONG, PW), F32), in...  55 us
    pallas_call x1, Pallas kernels, finish(): pl.pallas_call(filter_kernel, out_shape=(out, out), in_specs=[VMEM, VMEM]...  1.75 us

profile of v4, /device:TPU:56, one launch (start us, length us, event | category | flops | bytes accessed | tf_op | source)
XLA Modules:
  0.0 57.4 jit_solution(7863770480087122668)
XLA Ops:
  0.6 55.0 %exchange.1.sum_ref = f32[104,128]{1,0:T(8,128)S(1)} custom-call(s32[96]{0:T(128)} %kind_in.1, f32[14,40]{1,0:T(8,128)} %bitcast.4, s32[1,96]{1,0:T(1,128)} %bitcast.5, s32[1,96]{1,0:T(1,128)} %bitcast.6, bf16[1,96]{1,0:T(2,128)(2,1)} %bitcast.7, bf16[14,41]{1,0:T(8,128)(2,1)} %col_in.1, bf16[14,41]{1,0:T(8,128)(2,1)} %row_in.1, bf16[96,32,128]{2,1,0:T(8,128)(2,1)} %pieces_ref.1), custom_call_target="tpu_custom_call" | custom-call | tf_op jit(solution)/shard_map/exchange/pallas_call | solution.py:461
  55.7 1.8 %finish.1 = (f32[64,128]{1,0:T(8,128)}, f32[64,128]{1,0:T(8,128)}) custom-call(f32[104,128]{1,0:T(8,128)S(1)} %exchange.1.sum_ref, bf16[2,21]{1,0:T(2,128)(2,1)} %taps_ref.1), custom_call_target="tpu_custom_call" | custom-call | tf_op jit(solution)/shard_map/finish/pallas_call | solution.py:510

commit v5 on v4

--- a/solution.py
+++ b/solution.py
@@ -30,8 +30,10 @@
 META = 16
 ROWS = META + SLOTS * PR
 LONG = STRIP + 2 * HALO + 8
-CHUNKS = 4
-CHUNK_DESTS = 8 // CHUNKS
+PARTS = (3, 2, 2, 1)
+CHUNKS = len(PARTS)
+FIRST = tuple(sum(PARTS[:part]) for part in range(CHUNKS))
+EARLY = 2
 ORDER = (4, 3, 5, 2, 6, 1, 7, 0)
 
 
@@ -209,8 +211,8 @@
 
     def part_of(ref, at, part):
         if part == 0:
-            return ref.at[at, pl.ds(0, META + CHUNK_DESTS * 64)]
-        return ref.at[at, pl.ds(META + part * CHUNK_DESTS * 64, CHUNK_DESTS * 64)]
+            return ref.at[at, pl.ds(0, META + PARTS[0] * 64)]
+        return ref.at[at, pl.ds(META + FIRST[part] * 64, PARTS[part] * 64)]
 
     def a_copy(message, part, slot, target):
         return pltpu.make_async_remote_copy(
@@ -286,16 +288,16 @@
 
             @pl.loop(0, READY)
             def _(message):
-                for part in range(CHUNKS):
+                for part in range(EARLY):
                     send(message, part)
 
         @pl.when(group >= READY)
         def _():
-            for part in range(CHUNKS):
+            for part in range(EARLY):
                 send(group, part)
 
     for part in range(CHUNKS):
-        for message in range(groups, 16):
+        for message in range(groups if part < EARLY else 0, 16):
             if part == 0:
                 fill(message)
             send_fixed(message, part)
@@ -314,9 +316,12 @@
     def joined(tile):
         return tile + pltpu.roll(tile, 4, 0)
 
+    def strips_of(ref, at, part):
+        return ref.at[at, pl.ds(FIRST[part], PARTS[part])]
+
     def b_copy(part, at):
         return pltpu.make_async_remote_copy(
-            src_ref=sb.at[part, at], dst_ref=rbb.at[v, part],
+            src_ref=strips_of(sb, at, part), dst_ref=strips_of(rbb, v, part),
             send_sem=b_send.at[part, at], recv_sem=b_recv.at[part, v],
             device_id={"visit": at}, device_id_type=MESH,
         )
@@ -329,9 +334,8 @@
         if part == 0:
             mf[...] = rb[:, 0:META, :].astype(F32)
 
-        @pl.loop(0, CHUNK_DESTS)
-        def _(e):
-            j = part * CHUNK_DESTS + e
+        @pl.loop(FIRST[part], FIRST[part] + PARTS[part])
+        def _(j):
             total = jnp.zeros((PH, 2 * PW), F32)
             for four in range(4):
                 places = []
@@ -359,14 +363,16 @@
                     strip = jnp.concatenate([total[start:PH, 0:PW], edge], axis=0)
                 else:
                     strip = total[start:stop, 0:PW]
-                sb[part, at, e, 0:SPAN, :] = strip.astype(BF16)
-                sb[part, at, e, SPAN:, :] = tile
+                sb[at, j, 0:SPAN, :] = strip.astype(BF16)
+                sb[at, j, SPAN:, :] = tile
 
         @pl.loop(1, VISITS)
         def _(i):
             b_copy(part, lax.rem(v + i, VISITS)).start()
 
-        pltpu.make_async_copy(sb.at[part, v], rbb.at[v, part], b_recv.at[part, v]).start()
+        pltpu.make_async_copy(
+            strips_of(sb, v, part), strips_of(rbb, v, part), b_recv.at[part, v]
+        ).start()
 
     def c_copy(j):
         return pltpu.make_async_remote_copy(
@@ -378,13 +384,14 @@
 
     def collect(part):
         for at in range(VISITS):
-            pltpu.make_async_copy(rbb.at[at, part], rbb.at[at, part], b_recv.at[part, at]).wait()
-
-        for e in range(CHUNK_DESTS):
-            j = part * CHUNK_DESTS + e
-            total = rbb[0, part, e].astype(F32)
+            pltpu.make_async_copy(
+                strips_of(rbb, at, part), strips_of(rbb, at, part), b_recv.at[part, at]
+            ).wait()
+
+        for j in range(FIRST[part], FIRST[part] + PARTS[part]):
+            total = rbb[0, j].astype(F32)
             for at in range(1, VISITS):
-                total = total + rbb[at, part, e].astype(F32)
+                total = total + rbb[at, j].astype(F32)
             sc[j, 0:SPAN, :] = total[0:SPAN].astype(BF16)
             sc[j, SPAN:, :] = split(joined(total[SPAN:])).astype(BF16)
 
@@ -483,8 +490,8 @@
             pltpu.VMEM((16, ROWS, PW), BF16),
             pltpu.VMEM((16, ROWS, PW), BF16),
             pltpu.VMEM((16, META, PW), F32),
-            pltpu.VMEM((CHUNKS, VISITS, CHUNK_DESTS, LONG, PW), BF16),
-            pltpu.VMEM((VISITS, CHUNKS, CHUNK_DESTS, LONG, PW), BF16),
+            pltpu.VMEM((VISITS, SIDE, LONG, PW), BF16),
+            pltpu.VMEM((VISITS, SIDE, LONG, PW), BF16),
             pltpu.VMEM((SIDE, LONG, PW), BF16),
             pltpu.VMEM((SIDE, LONG, PW), BF16),
             dma((7,)),

time: 57.6 us -> 54.4 us (0.944)
  Pallas kernels: 56.8 us -> 53.6 us
    pallas_call x1, Pallas kernels: 55 us -> 51.8 us  [exchange(): pl.pallas_call(exchange_kernel, out_shape=pltpu.VMEM((LONG, PW), F32), in...]
where the time goes in v5:
time: 54.4 us; the launch traced here: 54.2 us
  Pallas kernels  53.6 us (99%)
  between operations  0.64 us (1%)
    pallas_call x1, Pallas kernels, exchange(): pl.pallas_call(exchange_kernel, out_shape=pltpu.VMEM((LONG, PW), F32), in...  51.8 us
    pallas_call x1, Pallas kernels, finish(): pl.pallas_call(filter_kernel, out_shape=(out, out), in_specs=[VMEM, VMEM]...  1.75 us

profile of v5, /device:TPU:56, one launch (start us, length us, event | category | flops | bytes accessed | tf_op | source)
XLA Modules:
  0.0 54.2 jit_solution(18246070140495049146)
XLA Ops:
  0.6 51.8 %exchange.1.sum_ref = f32[104,128]{1,0:T(8,128)S(1)} custom-call(s32[96]{0:T(128)} %kind_in.1, f32[14,40]{1,0:T(8,128)} %bitcast.4, s32[1,96]{1,0:T(1,128)} %bitcast.5, s32[1,96]{1,0:T(1,128)} %bitcast.6, bf16[1,96]{1,0:T(2,128)(2,1)} %bitcast.7, bf16[14,41]{1,0:T(8,128)(2,1)} %col_in.1, bf16[14,41]{1,0:T(8,128)(2,1)} %row_in.1, bf16[96,32,128]{2,1,0:T(8,128)(2,1)} %pieces_ref.1), custom_call_target="tpu_custom_call" | custom-call | tf_op jit(solution)/shard_map/exchange/pallas_call | solution.py:468
  52.5 1.8 %finish.1 = (f32[64,128]{1,0:T(8,128)}, f32[64,128]{1,0:T(8,128)}) custom-call(f32[104,128]{1,0:T(8,128)S(1)} %exchange.1.sum_ref, bf16[2,21]{1,0:T(2,128)(2,1)} %taps_ref.1), custom_call_target="tpu_custom_call" | custom-call | tf_op jit(solution)/shard_map/finish/pallas_call | solution.py:517

commit v6 on v5

--- a/solution.py
+++ b/solution.py
@@ -21,7 +21,7 @@
 TD = 21
 SIDE = 8
 VISITS = 4
-READY = 1
+READY = 0
 GROUP = 16
 STRIP = PH // VISITS
 HALO = 16
@@ -65,6 +65,21 @@
         r = jnp.where(row_band, r, 0.0)
         r = r + pltpu.roll(r, 32, 1) + pltpu.roll(r, 64, 1) + pltpu.roll(r, 96, 1)
         r_ref[b] = r.reshape(4, 8, PW)
+
+
+def filters(taps_ref, pad_ref, cols_ref, rows_ref):
+    half = TD // 2
+    pad_ref[...] = jnp.zeros_like(pad_ref)
+    pad_ref[0:2, 6 : 6 + TD] = taps_ref[...].astype(F32)
+    square = (PW, PW)
+    taps = jnp.broadcast_to(pad_ref[1:2, :], square)
+    cols = pltpu.roll(taps, PW - half - 6, 1, stride=1, stride_axis=0)
+    cols_ref[...] = jnp.where(
+        jnp.abs(iota(square, 1) - iota(square, 0)) <= half, cols, 0.0
+    ).astype(BF16)
+    taps = jnp.broadcast_to(pad_ref[0:1, :], (STRIP, PW))
+    rows = pltpu.roll(taps, HALO - half - 6, 1, stride=1, stride_axis=0)
+    rows_ref[...] = rows.astype(BF16)
 
 
 def plan(y, z, c, dest_ref, off_ref, weight_ref, plan_ref, padf_ref, stage_ref):
@@ -150,8 +165,9 @@
 
 
 def exchange_kernel(
-    kind_in, coef_in, dest_in, off_in, weight_in, col_in, row_in, pieces_ref,
-    sum_ref,
+    kind_in, coef_in, dest_in, off_in, weight_in, col_in, row_in, taps_in, pieces_ref,
+    coadd_ref, detection_ref,
+    sum_ref, den_ref, cols_ref, rows_ref, taps_ref,
     kind_s, coef_s, dest_ref, off_ref, weight_ref, col_ref, row_ref, x, g_ref, r_ref, y_ref, pad_ref, padf_ref, plan_ref, plan_s, matched_ref, stage_ref,
     rb, mf, sb, rbb, sc, rc,
     in_sem, x_sem, plan_sem, a_send, a_recv, b_send, b_recv, c_send, c_recv,
@@ -172,6 +188,7 @@
             (
                 (dest_in, dest_ref), (off_in, off_ref), (weight_in, weight_ref),
                 (col_in, col_ref), (row_in, row_ref), (kind_in, kind_s), (coef_in, coef_s),
+                (taps_in, taps_ref),
             )
         )
     ]
@@ -205,6 +222,8 @@
     plan_copy = pltpu.make_async_copy(plan_ref, plan_s, plan_sem)
     plan_copy.start()
     tables(col_ref, row_ref, pad_ref, g_ref, r_ref)
+    filters(taps_ref, pad_ref, cols_ref, rows_ref)
+    den_ref[...] = jnp.zeros_like(den_ref)
     matched_ref[PIECES:, :, :] = jnp.zeros((8, PR, PW), BF16)
     plan_copy.wait()
     x_copy.wait()
@@ -425,8 +444,16 @@
     for i in range(SIDE):
         pltpu.make_async_copy(rc.at[i], rc.at[i], c_recv.at[i]).wait()
         total = total + rc[i].astype(F32)
-    sum_ref[0:SPAN, :] = total[0:SPAN]
-    sum_ref[SPAN:, :] = joined(total[SPAN:])
+    sum_ref[...] = joined(total[SPAN:])
+    for a in range(2):
+        column = jnp.broadcast_to(sum_ref[a : a + 1, :], (PW, PW)).T
+        den_ref[HALO + a * PW : HALO + (a + 1) * PW, :] = column
+    den = den_ref[pl.ds(pl.multiple_of(v * STRIP, STRIP), SPAN), :]
+    coadd = total[0:SPAN] / (1.0 + den)
+    coadd_ref[...] = coadd[HALO : HALO + STRIP]
+    smoothed = jnp.dot(coadd.astype(BF16), cols_ref[...], preferred_element_type=F32).astype(BF16)
+    smoothed = jnp.concatenate([smoothed, jnp.zeros((PW - SPAN, PW), BF16)], axis=0)
+    detection_ref[...] = jnp.dot(rows_ref[...], smoothed, preferred_element_type=F32)
 
     @pl.loop(0, SIDE)
     def _(j):
@@ -435,42 +462,25 @@
             c_copy(j).wait_send()
 
 
-def filter_kernel(sum_ref, taps_ref, coadd_ref, detection_ref, den_ref, pad_ref):
-    v = lax.axis_index("visit")
-    half = TD // 2
-    pad_ref[...] = jnp.zeros_like(pad_ref)
-    pad_ref[0:2, 6 : 6 + TD] = taps_ref[...].astype(F32)
-    square = (PW, PW)
-    lane, row = iota(square, 1), iota(square, 0)
-    taps = jnp.broadcast_to(pad_ref[1:2, :], square)
-    cols = pltpu.roll(taps, PW - half - 6, 1, stride=1, stride_axis=0)
-    cols = jnp.where(jnp.abs(lane - row) <= half, cols, 0.0).astype(BF16)
-    taps = jnp.broadcast_to(pad_ref[0:1, :], (STRIP, PW))
-    rows = pltpu.roll(taps, HALO - half - 6, 1, stride=1, stride_axis=0).astype(BF16)
-    den_ref[...] = jnp.zeros_like(den_ref)
-    for a in range(2):
-        column = jnp.broadcast_to(sum_ref[SPAN + a : SPAN + a + 1, :], square).T
-        den_ref[HALO + a * PW : HALO + (a + 1) * PW, :] = column
-    den = den_ref[pl.ds(pl.multiple_of(v * STRIP, STRIP), SPAN), :]
-    coadd = sum_ref[0:SPAN, :] / (1.0 + den)
-    coadd_ref[...] = coadd[HALO : HALO + STRIP]
-    smoothed = jnp.dot(coadd.astype(BF16), cols, preferred_element_type=F32).astype(BF16)
-    smoothed = jnp.concatenate([smoothed, jnp.zeros((PW - SPAN, PW), BF16)], axis=0)
-    detection_ref[...] = jnp.dot(rows, smoothed, preferred_element_type=F32)
-
-
 VMEM = pl.BlockSpec(memory_space=pltpu.VMEM)
 
 
-def exchange(pieces, dest, offsets, kernel_index, weights, basis_col, basis_row, coef_table):
+def exchange(
+    pieces, dest, offsets, kernel_index, weights, basis_col, basis_row, coef_table, det_taps
+):
     dma = pltpu.SemaphoreType.DMA
     row = (1, PIECES)
     return pl.pallas_call(
         exchange_kernel,
-        out_shape=pltpu.VMEM((LONG, PW), F32),
-        in_specs=[pl.BlockSpec(memory_space=pl.ANY)] * 8,
-        out_specs=VMEM,
+        out_shape=(pltpu.VMEM((STRIP, PW), F32), pltpu.VMEM((STRIP, PW), F32)),
+        in_specs=[pl.BlockSpec(memory_space=pl.ANY)] * 9,
+        out_specs=(VMEM, VMEM),
         scratch_shapes=[
+            pltpu.VMEM((8, PW), F32),
+            pltpu.VMEM((PH + 2 * HALO, PW), F32),
+            pltpu.VMEM((PW, PW), BF16),
+            pltpu.VMEM((STRIP, PW), BF16),
+            pltpu.VMEM(det_taps.shape, BF16),
             pltpu.SMEM((PIECES,), I32),
             pltpu.SMEM(coef_table.shape[::-1], F32),
             pltpu.VMEM(row, I32),
@@ -494,7 +504,7 @@
             pltpu.VMEM((VISITS, SIDE, LONG, PW), BF16),
             pltpu.VMEM((SIDE, LONG, PW), BF16),
             pltpu.VMEM((SIDE, LONG, PW), BF16),
-            dma((7,)),
+            dma((8,)),
             dma(()),
             dma(()),
             dma((CHUNKS, 16)),
@@ -508,29 +518,16 @@
         name="exchange",
     )(
         kernel_index, coef_table.T, dest.reshape(row), offsets.reshape(row), weights.reshape(row),
-        basis_col, basis_row, pieces,
+        basis_col, basis_row, det_taps, pieces,
     )
-
-
-def finish(sums, det_taps):
-    out = jax.ShapeDtypeStruct((STRIP, PW), F32)
-    return pl.pallas_call(
-        filter_kernel,
-        out_shape=(out, out),
-        in_specs=[VMEM, VMEM],
-        out_specs=(VMEM, VMEM),
-        scratch_shapes=[pltpu.VMEM((PH + 2 * HALO, PW), F32), pltpu.VMEM((8, PW), F32)],
-        name="finish",
-    )(pltpu.with_memory_space_constraint(sums, pltpu.VMEM), det_taps)
 
 
 def shards(
     pieces, dest, offsets, kernel_index, weights, basis_col, basis_row, coef_table, det_taps
 ):
-    sums = exchange(
-        pieces, dest, offsets, kernel_index, weights, basis_col, basis_row, coef_table
+    return exchange(
+        pieces, dest, offsets, kernel_index, weights, basis_col, basis_row, coef_table, det_taps
     )
-    return finish(sums, det_taps)
 
 
 def solution(mesh):

time: 54.4 us -> 53.8 us (0.989)
  Pallas kernels: 53.6 us -> 51.8 us
  local copies, waits for them, and re-layouts: 0 us -> 1.23 us
    pallas_call x2 -> x1, Pallas kernels: 53.6 us -> 51.8 us  [exchange(): pl.pallas_call(exchange_kernel, out_shape=(pltpu.VMEM((STRIP, PW), F32),...]
    unnamed x0 -> x2, local copies, waits for them, and re-layouts: none -> 1.23 us
where the time goes in v6:
time: 53.8 us; the launch traced here: 53.6 us
  Pallas kernels  51.8 us (96%)
  local copies, waits for them, and re-layouts  1.23 us (2%)
  between operations  0.64 us (1%)
    pallas_call x1, Pallas kernels, exchange(): pl.pallas_call(exchange_kernel, out_shape=(pltpu.VMEM((STRIP, PW), F32),...  51.8 us
    unnamed x2, local copies, waits for them, and re-layouts  1.23 us

profile of v6, /device:TPU:56, one launch (start us, length us, event | category | flops | bytes accessed | tf_op | source)
XLA Modules:
  0.0 53.6 jit_solution(13680828893467641414)
XLA Ops:
  0.6 51.8 %exchange.1 = (f32[64,128]{1,0:T(8,128)S(1)}, f32[64,128]{1,0:T(8,128)S(1)}) custom-call(s32[96]{0:T(128)} %kind_in.1, f32[14,40]{1,0:T(8,128)} %bitcast.4, s32[1,96]{1,0:T(1,128)} %bitcast.5, s32[1,96]{1,0:T(1,128)} %bitcast.6, bf16[1,96]{1,0:T(2,128)(2,1)} %bitcast.7, bf16[14,41]{1,0:T(8,128)(2,1)} %col_in.1, bf16[14,41]{1,0:T(8,128)(2,1)} %row_in.1, ...), custom_call_target="tpu_custom_call" | custom-call | tf_op jit(solution)/shard_map/exchange/pallas_call | solution.py:473
  52.4 0.6 %copy.13 = f32[64,128]{1,0:T(8,128)} copy(f32[64,128]{1,0:T(8,128)S(1)} %get-tuple-element.2) | data formatting | bytes 65536
  53.0 0.6 %copy.14 = f32[64,128]{1,0:T(8,128)} copy(f32[64,128]{1,0:T(8,128)S(1)} %get-tuple-element.3) | data formatting | bytes 65536

commit v7 on v6

--- a/solution.py
+++ b/solution.py
@@ -30,10 +30,10 @@
 META = 16
 ROWS = META + SLOTS * PR
 LONG = STRIP + 2 * HALO + 8
-PARTS = (3, 2, 2, 1)
+PARTS = (4, 2, 2)
 CHUNKS = len(PARTS)
 FIRST = tuple(sum(PARTS[:part]) for part in range(CHUNKS))
-EARLY = 2
+EARLY = 1
 ORDER = (4, 3, 5, 2, 6, 1, 7, 0)
 
 

time: 53.8 us -> 53.6 us (level)
  no operation moved by 1% of the time
where the time goes in v7:
time: 53.6 us; the launch traced here: 53.4 us
  Pallas kernels  51.5 us (96%)
  local copies, waits for them, and re-layouts  1.23 us (2%)
  between operations  0.64 us (1%)
    pallas_call x1, Pallas kernels, exchange(): pl.pallas_call(exchange_kernel, out_shape=(pltpu.VMEM((STRIP, PW), F32),...  51.5 us
    unnamed x2, local copies, waits for them, and re-layouts  1.23 us

profile of v7, /device:TPU:56, one launch (start us, length us, event | category | flops | bytes accessed | tf_op | source)
XLA Modules:
  0.0 53.4 jit_solution(14611098212556347183)
XLA Ops:
  0.6 51.5 %exchange.1 = (f32[64,128]{1,0:T(8,128)S(1)}, f32[64,128]{1,0:T(8,128)S(1)}) custom-call(s32[96]{0:T(128)} %kind_in.1, f32[14,40]{1,0:T(8,128)} %bitcast.4, s32[1,96]{1,0:T(1,128)} %bitcast.5, s32[1,96]{1,0:T(1,128)} %bitcast.6, bf16[1,96]{1,0:T(2,128)(2,1)} %bitcast.7, bf16[14,41]{1,0:T(8,128)(2,1)} %col_in.1, bf16[14,41]{1,0:T(8,128)(2,1)} %row_in.1, ...), custom_call_target="tpu_custom_call" | custom-call | tf_op jit(solution)/shard_map/exchange/pallas_call | solution.py:473
  52.2 0.6 %copy.13 = f32[64,128]{1,0:T(8,128)} copy(f32[64,128]{1,0:T(8,128)S(1)} %get-tuple-element.2) | data formatting | bytes 65536
  52.8 0.6 %copy.14 = f32[64,128]{1,0:T(8,128)} copy(f32[64,128]{1,0:T(8,128)S(1)} %get-tuple-element.3) | data formatting | bytes 65536
